TPU v7x, 1024 devices: a whole 4x8x16 slice. The times are simulated.
1024 devices in a mesh: stream: 256 (over y, z, core), span: 4 (over x).
Axes of the slice: x: 4, y: 8, z: 16, core: 2. Of those that a mesh axis runs over, the one named last changes fastest.
Arguments:
- basis: float32 [4, 10, 2048, 8, 512], P(None, None, 'stream', None, 'span'), may hold values from -6 to 6
- coeffs: float32 [4], replicated, may hold values from -3 to 3
- mixing_matrix: float32 [10, 10], replicated, may hold values from -2 to 2
- base_speed: float32 [2048, 8, 512], P('stream', None, 'span'), may hold values from 0.5 to 1.5
- span_speed: float32 [2048, 8, 512], P('stream', None, 'span'), may hold values from -2.4 to 2.4
- polymer_gain: float32 [2048, 8, 512], P('stream', None, 'span'), may hold values from 0.3 to 3
Outputs:
- proj: float32 [4, 4], replicated
- rfactor: float32 [4, 4], replicated
- basis_new: float32 [4, 10, 2048, 8, 512], P(None, None, 'stream', None, 'span')
All inputs are finite; a program needn't handle non-finite values.
Results may differ from a plain program's by a relative error of at most 0.00025.
Values sent between devices are 32-bit elements; how exact they have to be, the bound alone decides.
No kernel may reach another device: no remote copies, remote signals or barrier semaphores. Data moves between devices by JAX's collectives and lax.ppermute only.
A program may use at most 32 MiB of HBM per device.

v0:
```python
import jax
import jax.numpy as jnp
from jax import lax
from jax.sharding import PartitionSpec as P

STEPS = 4


def padded(value, sides, width):
    for axis, dim in sides:
        size, length = (lax.axis_size(axis), value.shape[dim])
        up = [(i, (i + 1) % size) for i in range(size)]
        down = [(j, i) for i, j in up]
        last = lax.slice_in_dim(value, length - width, length, axis=dim)
        leading = lax.slice_in_dim(value, 0, width, axis=dim)
        before = lax.ppermute(last, axis, up)
        after = lax.ppermute(leading, axis, down)
        value = jnp.concatenate([before, value, after], axis=dim)
    return value


def advance(values_now, base_speed, span_speed, polymer_gain, mixing_matrix):
    center_part = values_now[:, 1:-1, :, 1:-1]
    forward_x = values_now[:, 2:, :, 1:-1]
    backward_x = values_now[:, :-2, :, 1:-1]
    forward_z = values_now[:, 1:-1, :, 2:]
    backward_z = values_now[:, 1:-1, :, :-2]
    zero_row = jnp.zeros_like(center_part[:, :, :1, :])
    wall_up = jnp.concatenate([center_part[:, :, 1:, :], zero_row], axis=2)
    wall_down = jnp.concatenate([zero_row, center_part[:, :, :-1, :]], axis=2)
    laplace = (
        forward_x + backward_x + forward_z + backward_z + wall_up + wall_down - 6.0 * center_part
    )
    mixing = jnp.einsum(
        "fg,gxyz->fxyz", mixing_matrix, center_part, precision=lax.Precision.HIGHEST
    )
    return (
        -base_speed * (forward_x - backward_x) * 0.5
        - span_speed * (forward_z - backward_z) * 0.5
        + 0.05 * laplace
        + polymer_gain * mixing
    )


def on_device(basis, coeffs, mixing_matrix, base_speed, span_speed, polymer_gain):
    total = float(basis[0].size * lax.axis_size("stream") * lax.axis_size("span"))
    start = jnp.einsum("m,mfxyz->fxyz", coeffs, basis, precision=lax.Precision.HIGHEST)
    krylov = []
    current = start
    for section in range(STEPS):
        rimmed = padded(current, (("stream", 1), ("span", 3)), 1)
        current = advance(rimmed, base_speed, span_speed, polymer_gain, mixing_matrix)
        krylov.append(current)
    stacked = jnp.stack(krylov, 0)
    flat_basis = basis.reshape(basis.shape[0], -1)
    flat_new = stacked.reshape(STEPS, -1)
    local_proj = jnp.dot(flat_basis, flat_new.T, precision=lax.Precision.HIGHEST)
    proj = lax.psum(local_proj, ("stream", "span")) / total
    projected = flat_new - jnp.dot(proj.T, flat_basis, precision=lax.Precision.HIGHEST)
    local_gram = jnp.dot(projected, projected.T, precision=lax.Precision.HIGHEST)
    gram = lax.psum(local_gram, ("stream", "span")) / total
    lower_factor = jnp.linalg.cholesky(gram)
    solved = jax.scipy.linalg.solve_triangular(lower_factor, projected, lower=True)
    return (proj, lower_factor.T, solved.reshape(stacked.shape))


def solution(mesh):
    placed = (
        P(None, None, "stream", None, "span"),
        P(),
        P(),
        P("stream", None, "span"),
        P("stream", None, "span"),
        P("stream", None, "span"),
    )
    return jax.shard_map(
        on_device,
        mesh=mesh,
        in_specs=placed,
        out_specs=(P(), P(), P(None, None, "stream", None, "span")),
        check_vma=False,
    )
```

profile of v0, /device:TPU:1, one launch (start us, length us, event | category | flops | bytes accessed | tf_op | source)
XLA Modules:
  0.0 385.3 jit_solution(10839615956824409071)
XLA Ops:
  0.6 4.3 %fusion.12 = f32[1,10,8,8,128]{4,0,3,2,1:T(1,128)S(1)} fusion(f32[4,10,8,8,128]{4,3,2,1,0:T(8,128)} %param.6, f32[4]{0:T(128)} %param.7), kind=kOutput, calls=%fused_computation.18 | convolution fusion | flops 3932160 | bytes 1638416 | tf_op jit(solution)/shard_map/m,mfxyz->fxyz/dot_general | solution.py:47
  5.1 16.1 %collective-permute-start = (f32[10,1,8,128]{3,0,2,1:T(8,128)S(1)}, f32[10,1,8,128]{3,0,2,1:T(8,128)S(1)}, u32[]{:S(2)}, u32[]{:S(2)}) collective-permute-start(f32[10,1,8,128]{3,0,2,1:T(8,128)S(1)} %get-tuple-element.33), channel_id=1, source_target_pairs={{4,0},{8,4},{12,8},{16,12},{20,16},{24,20},{28,24},{32,28},{36,32}... | collective-permute-start | bytes 122888 | tf_op jit(solution)/shard_map/ppermute | solution.py:17
  21.2 1.9 collective-permute-start.1
  23.2 6.7 %collective-permute-done.1 = f32[10,1,8,128]{3,0,2,1:T(8,128)S(1)} collective-permute-done((f32[10,1,8,128]{3,0,2,1:T(8,128)S(1)}, f32[10,1,8,128]{3,0,2,1:T(8,128)S(1)}, u32[]{:S(2)}, u32[]{:S(2)}) %collective-permute-start.1) | collective-permute-done | bytes 40992 | tf_op jit(solution)/shard_map/ppermute | solution.py:16
  30.8 4.5 %collective-permute-start.2 = (f32[10,10,8,1]{1,2,3,0:T(8,128)S(1)}, f32[10,10,8,1]{1,2,3,0:T(8,128)S(1)}, u32[]{:S(2)}, u32[]{:S(2)}) collective-permute-start(f32[10,10,8,1]{1,2,3,0:T(8,128)S(1)} %copy.31), channel_id=1, source_target_pairs={{1,0},{2,1},{3,2},{0,3},{5,4},{6,5},{7,6},{4,7},{9,8},{10,9},{11,1... | collective-permute-start | bytes 9608 | tf_op jit(solution)/shard_map/ppermute | solution.py:17
  35.9 2.1 collective-permute-start.3
  39.0 2.9 collective-permute-done.3
  43.9 9.6 %collective-permute-start.4 = (f32[10,1,8,128]{3,0,2,1:T(8,128)S(1)}, f32[10,1,8,128]{3,0,2,1:T(8,128)S(1)}, u32[]{:S(2)}, u32[]{:S(2)}) collective-permute-start(f32[10,1,8,128]{3,0,2,1:T(8,128)S(1)} %get-tuple-element.29), channel_id=1, source_target_pairs={{4,0},{8,4},{12,8},{16,12},{20,16},{24,20},{28,24},{32,28},{36,32}... | collective-permute-start | bytes 122888 | tf_op jit(solution)/shard_map/ppermute | solution.py:17
  53.5 1.9 collective-permute-start.5
  60.2 3.4 collective-permute-start.7
  68.1 8.7 %collective-permute-start.8 = (f32[10,1,8,128]{3,0,2,1:T(8,128)S(1)}, f32[10,1,8,128]{3,0,2,1:T(8,128)S(1)}, u32[]{:S(2)}, u32[]{:S(2)}) collective-permute-start(f32[10,1,8,128]{3,0,2,1:T(8,128)S(1)} %get-tuple-element.25), channel_id=1, source_target_pairs={{4,0},{8,4},{12,8},{16,12},{20,16},{24,20},{28,24},{32,28},{36,32}... | collective-permute-start | bytes 122888 | tf_op jit(solution)/shard_map/ppermute | solution.py:17
  76.8 1.9 collective-permute-start.9
  83.5 3.5 collective-permute-start.11
  90.4 1.9 fusion.7
  92.4 8.7 %collective-permute-start.12 = (f32[10,1,8,128]{3,0,2,1:T(8,128)S(1)}, f32[10,1,8,128]{3,0,2,1:T(8,128)S(1)}, u32[]{:S(2)}, u32[]{:S(2)}) collective-permute-start(f32[10,1,8,128]{3,0,2,1:T(8,128)S(1)} %get-tuple-element.21), channel_id=1, source_target_pairs={{4,0},{8,4},{12,8},{16,12},{20,16},{24,20},{28,24},{32,28},{36,32}... | collective-permute-start | bytes 122888 | tf_op jit(solution)/shard_map/ppermute | solution.py:17
  101.1 1.9 collective-permute-start.13
  108.1 3.4 collective-permute-start.15
  115.1 2.0 fusion.5
  118.4 6.8 %fusion.15 = f32[4,4]{0,1:T(4,128)S(1)} fusion(f32[4,10,8,8,128]{4,3,2,1,0:T(8,128)S(1)} %copy-done.1, f32[4,10,8,8,128]{4,1,3,2,0:T(8,128)S(1)} %pad_maximum_fusion), kind=kOutput, calls=%fused_computation.21 | convolution fusion | flops 15728640 | bytes 2621504 | tf_op jit(solution)/shard_map/dot_general | solution.py:57
  126.0 122.6 %psum.14 = f32[4,4]{0,1:T(4,128)S(1)} all-reduce(f32[4,4]{0,1:T(4,128)S(1)} %fusion.15), channel_id=1, replica_groups=mesh['stream'=256,'span'=4] {'stream','span'}, use_global_device_ids=true, to_apply=%region_0.0 | all-reduce | flops 16 | bytes 128 | tf_op jit(solution)/shard_map/psum | solution.py:58
  248.7 5.4 %convolution_subtract_fusion = f32[4,81920]{1,0:T(4,128)S(1)} fusion(f32[1,4,640,128]{3,2,1,0:T(8,128)S(1)} %bitcast.88, f32[1,81920]{1,0:T(1,128)} %bitcast.93, f32[1,81920]{1,0:T(1,128)} %bitcast.92, f32[1,81920]{1,0:T(1,128)S(1)} %bitcast.91, f32[1,81920]{1,0:T(1,128)S(1)} %bitcast.90, f32[4,4]{0,1:T(4,128)S(1)} %psum.14), kind=kOutput, calls=%fused_computation | convolution fusion | flops 17039376 | bytes 3932224 | tf_op jit(solution)/shard_map/dot_general | solution.py:59
  254.0 5.7 %fusion.41 = f32[4,4]{0,1:T(4,128)S(1)} fusion(f32[4,81920]{1,0:T(4,128)S(1)} %convolution_subtract_fusion), kind=kOutput, calls=%fused_computation.89 | convolution fusion | flops 15728640 | bytes 1310784 | tf_op jit(solution)/shard_map/dot_general | solution.py:60
  259.7 118.1 %psum.15 = f32[4,4]{0,1:T(4,128)S(1)} all-reduce(f32[4,4]{0,1:T(4,128)S(1)} %fusion.41), channel_id=1, replica_groups=mesh['stream'=256,'span'=4] {'stream','span'}, use_global_device_ids=true, to_apply=%region_1.0 | all-reduce | flops 16 | bytes 128 | tf_op jit(solution)/shard_map/psum | solution.py:61
  380.0 2.8 fusion.24
  (84 shorter events, 37.5 us)
Async XLA Ops:
  0.6 42.3 %copy-start = (f32[10,10]{1,0:T(8,128)S(1)}, f32[10,10]{1,0:T(8,128)}, u32[]{:S(2)}) copy-start(f32[10,10]{1,0:T(8,128)} %param.8) | copy-start | bytes 1204
  5.1 18.0 %collective-permute-start = (f32[10,1,8,128]{3,0,2,1:T(8,128)S(1)}, f32[10,1,8,128]{3,0,2,1:T(8,128)S(1)}, u32[]{:S(2)}, u32[]{:S(2)}) collective-permute-start(f32[10,1,8,128]{3,0,2,1:T(8,128)S(1)} %get-tuple-element.33), channel_id=1, source_target_pairs={{4,0},{8,4},{12,8},{16,12},{20,16},{24,20},{28,24},{32,28},{36,32}... | collective-permute-start | bytes 122888 | tf_op jit(solution)/shard_map/ppermute | solution.py:17
  21.2 8.7 %collective-permute-start.1 = (f32[10,1,8,128]{3,0,2,1:T(8,128)S(1)}, f32[10,1,8,128]{3,0,2,1:T(8,128)S(1)}, u32[]{:S(2)}, u32[]{:S(2)}) collective-permute-start(f32[10,1,8,128]{3,0,2,1:T(8,128)S(1)} %get-tuple-element.32), channel_id=1, source_target_pairs={{0,4},{4,8},{8,12},{12,16},{16,20},{20,24},{24,28},{28,32},{32,36}... | collective-permute-start | bytes 122888 | tf_op jit(solution)/shard_map/ppermute | solution.py:16
  30.8 7.3 %copy-start.4 = (f32[8,8,128]{2,1,0:T(8,128)S(1)}, f32[8,8,128]{2,1,0:T(8,128)}, u32[]{:S(2)}) copy-start(f32[8,8,128]{2,1,0:T(8,128)} %param.9) | copy-start | bytes 98308
  30.8 7.3 %collective-permute-start.2 = (f32[10,10,8,1]{1,2,3,0:T(8,128)S(1)}, f32[10,10,8,1]{1,2,3,0:T(8,128)S(1)}, u32[]{:S(2)}, u32[]{:S(2)}) collective-permute-start(f32[10,10,8,1]{1,2,3,0:T(8,128)S(1)} %copy.31), channel_id=1, source_target_pairs={{1,0},{2,1},{3,2},{0,3},{5,4},{6,5},{7,6},{4,7},{9,8},{10,9},{11,1... | collective-permute-start | bytes 9608 | tf_op jit(solution)/shard_map/ppermute | solution.py:17
  35.9 7.1 %copy-start.5 = (f32[8,8,128]{2,1,0:T(8,128)S(1)}, f32[8,8,128]{2,1,0:T(8,128)}, u32[]{:S(2)}) copy-start(f32[8,8,128]{2,1,0:T(8,128)} %param.11) | copy-start | bytes 98308
  35.9 7.1 %copy-start.6 = (f32[8,8,128]{2,1,0:T(8,128)S(1)}, f32[8,8,128]{2,1,0:T(8,128)}, u32[]{:S(2)}) copy-start(f32[8,8,128]{2,1,0:T(8,128)} %param.10) | copy-start | bytes 98308
  35.9 6.1 %collective-permute-start.3 = (f32[10,10,8,1]{1,2,3,0:T(8,128)S(1)}, f32[10,10,8,1]{1,2,3,0:T(8,128)S(1)}, u32[]{:S(2)}, u32[]{:S(2)}) collective-permute-start(f32[10,10,8,1]{1,2,3,0:T(8,128)S(1)} %copy.33), channel_id=1, source_target_pairs={{0,1},{1,2},{2,3},{3,0},{4,5},{5,6},{6,7},{7,4},{8,9},{9,10},{10,1... | collective-permute-start | bytes 9608 | tf_op jit(solution)/shard_map/ppermute | solution.py:16
  43.9 11.5 %collective-permute-start.4 = (f32[10,1,8,128]{3,0,2,1:T(8,128)S(1)}, f32[10,1,8,128]{3,0,2,1:T(8,128)S(1)}, u32[]{:S(2)}, u32[]{:S(2)}) collective-permute-start(f32[10,1,8,128]{3,0,2,1:T(8,128)S(1)} %get-tuple-element.29), channel_id=1, source_target_pairs={{4,0},{8,4},{12,8},{16,12},{20,16},{24,20},{28,24},{32,28},{36,32}... | collective-permute-start | bytes 122888 | tf_op jit(solution)/shard_map/ppermute | solution.py:17
  53.5 3.2 collective-permute-start.5
  57.7 6.0 %collective-permute-start.6 = (f32[10,10,8,1]{1,2,3,0:T(8,128)S(1)}, f32[10,10,8,1]{1,2,3,0:T(8,128)S(1)}, u32[]{:S(2)}, u32[]{:S(2)}) collective-permute-start(f32[10,10,8,1]{1,2,3,0:T(8,128)S(1)} %copy.35), channel_id=1, source_target_pairs={{1,0},{2,1},{3,2},{0,3},{5,4},{6,5},{7,6},{4,7},{9,8},{10,9},{11,1... | collective-permute-start | bytes 9608 | tf_op jit(solution)/shard_map/ppermute | solution.py:17
  60.2 6.0 %collective-permute-start.7 = (f32[10,10,8,1]{1,2,3,0:T(8,128)S(1)}, f32[10,10,8,1]{1,2,3,0:T(8,128)S(1)}, u32[]{:S(2)}, u32[]{:S(2)}) collective-permute-start(f32[10,10,8,1]{1,2,3,0:T(8,128)S(1)} %copy.37), channel_id=1, source_target_pairs={{0,1},{1,2},{2,3},{3,0},{4,5},{5,6},{6,7},{7,4},{8,9},{9,10},{10,1... | collective-permute-start | bytes 9608 | tf_op jit(solution)/shard_map/ppermute | solution.py:16
  68.1 10.7 %collective-permute-start.8 = (f32[10,1,8,128]{3,0,2,1:T(8,128)S(1)}, f32[10,1,8,128]{3,0,2,1:T(8,128)S(1)}, u32[]{:S(2)}, u32[]{:S(2)}) collective-permute-start(f32[10,1,8,128]{3,0,2,1:T(8,128)S(1)} %get-tuple-element.25), channel_id=1, source_target_pairs={{4,0},{8,4},{12,8},{16,12},{20,16},{24,20},{28,24},{32,28},{36,32}... | collective-permute-start | bytes 122888 | tf_op jit(solution)/shard_map/ppermute | solution.py:17
  76.8 3.2 collective-permute-start.9
  81.0 6.9 %collective-permute-start.10 = (f32[10,10,8,1]{1,2,3,0:T(8,128)S(1)}, f32[10,10,8,1]{1,2,3,0:T(8,128)S(1)}, u32[]{:S(2)}, u32[]{:S(2)}) collective-permute-start(f32[10,10,8,1]{1,2,3,0:T(8,128)S(1)} %copy.39), channel_id=1, source_target_pairs={{1,0},{2,1},{3,2},{0,3},{5,4},{6,5},{7,6},{4,7},{9,8},{10,9},{11,1... | collective-permute-start | bytes 9608 | tf_op jit(solution)/shard_map/ppermute | solution.py:17
  83.5 6.0 %collective-permute-start.11 = (f32[10,10,8,1]{1,2,3,0:T(8,128)S(1)}, f32[10,10,8,1]{1,2,3,0:T(8,128)S(1)}, u32[]{:S(2)}, u32[]{:S(2)}) collective-permute-start(f32[10,10,8,1]{1,2,3,0:T(8,128)S(1)} %copy.41), channel_id=1, source_target_pairs={{0,1},{1,2},{2,3},{3,0},{4,5},{5,6},{6,7},{7,4},{8,9},{9,10},{10,1... | collective-permute-start | bytes 9608 | tf_op jit(solution)/shard_map/ppermute | solution.py:16
  92.4 12.3 %collective-permute-start.12 = (f32[10,1,8,128]{3,0,2,1:T(8,128)S(1)}, f32[10,1,8,128]{3,0,2,1:T(8,128)S(1)}, u32[]{:S(2)}, u32[]{:S(2)}) collective-permute-start(f32[10,1,8,128]{3,0,2,1:T(8,128)S(1)} %get-tuple-element.21), channel_id=1, source_target_pairs={{4,0},{8,4},{12,8},{16,12},{20,16},{24,20},{28,24},{32,28},{36,32}... | collective-permute-start | bytes 122888 | tf_op jit(solution)/shard_map/ppermute | solution.py:17
  101.1 3.6 collective-permute-start.13
  105.6 7.6 %collective-permute-start.14 = (f32[10,10,8,1]{1,2,3,0:T(8,128)S(1)}, f32[10,10,8,1]{1,2,3,0:T(8,128)S(1)}, u32[]{:S(2)}, u32[]{:S(2)}) collective-permute-start(f32[10,10,8,1]{1,2,3,0:T(8,128)S(1)} %copy.43), channel_id=1, source_target_pairs={{1,0},{2,1},{3,2},{0,3},{5,4},{6,5},{7,6},{4,7},{9,8},{10,9},{11,1... | collective-permute-start | bytes 9608 | tf_op jit(solution)/shard_map/ppermute | solution.py:17
  108.1 6.0 %collective-permute-start.15 = (f32[10,10,8,1]{1,2,3,0:T(8,128)S(1)}, f32[10,10,8,1]{1,2,3,0:T(8,128)S(1)}, u32[]{:S(2)}, u32[]{:S(2)}) collective-permute-start(f32[10,10,8,1]{1,2,3,0:T(8,128)S(1)} %copy.45), channel_id=1, source_target_pairs={{0,1},{1,2},{2,3},{3,0},{4,5},{5,6},{6,7},{7,4},{8,9},{9,10},{10,1... | collective-permute-start | bytes 9608 | tf_op jit(solution)/shard_map/ppermute | solution.py:16
  117.1 1.3 copy-start.1
  118.4 130.2 %copy-start.2 = (f32[10,8,8,128]{3,2,1,0:T(8,128)S(1)}, f32[10,8,8,128]{3,2,1,0:T(8,128)}, u32[]{:S(2)}) copy-start(f32[10,8,8,128]{3,2,1,0:T(8,128)} %copy.49) | copy-start | bytes 983044
  118.4 130.2 %copy-start.3 = (f32[10,8,8,128]{3,2,1,0:T(8,128)S(1)}, f32[10,8,8,128]{3,2,1,0:T(8,128)}, u32[]{:S(2)}) copy-start(f32[10,8,8,128]{3,2,1,0:T(8,128)} %copy.50) | copy-start | bytes 983044
where the time goes:
time: 386 us; the launch traced here: 385 us
  blocking collectives  241 us (62%)
  starting transfers between devices  73.4 us (19%)
  matrix products  30.6 us (8%)
  local copies, waits for them, and re-layouts  22.8 us (6%)
  waiting for transfers between devices  14.4 us (4%)
    psum x1, blocking collectives, on_device(): proj = lax.psum(local_proj, ('stream', 'span')) / total  123 us
    psum x1, blocking collectives, on_device(): gram = lax.psum(local_gram, ('stream', 'span')) / total  118 us
    ppermute x8, starting transfers between devices, padded(): after = lax.ppermute(leading, axis, down)  53.4 us
    ppermute x8, starting transfers between devices, padded(): before = lax.ppermute(last, axis, up)  20 us
    ppermute x8, waiting for transfers between devices, padded(): before = lax.ppermute(last, axis, up)  14.4 us
  transfers between devices with their start and end apart: 16, of which 6 were waited for; matrix products, arithmetic and copies ran while one was open for 3% of the time, Pallas kernels for 0%

commit v1 on v0

v1 whole, which is shorter than its diff:
```python
import functools

import jax
import jax.numpy as jnp
import numpy as np
from jax import lax
from jax.experimental import pallas as pl
from jax.experimental.pallas import tpu as pltpu
from jax.sharding import Mesh
from jax.sharding import PartitionSpec as P

STEPS = 4
LANES = 128
EXTRA = 3
VMEM = pl.BlockSpec(memory_space=pltpu.VMEM)
SMEM = pl.BlockSpec(memory_space=pltpu.SMEM)
PAIRS = [(a, b) for a in range(STEPS) for b in range(a, STEPS)]


def lane_index():
    return lax.broadcasted_iota(jnp.int32, (8, LANES), 1)


def row_index():
    return lax.broadcasted_iota(jnp.int32, (8, LANES), 0)


def start_kernel(coeffs, basis, base_speed, span_speed, gain, low, high):
    count, fields = basis.shape[0], basis.shape[1]

    def field(f, carry):
        for x in range(2 * STEPS):
            value = coeffs[0] * basis[0, f, x]
            for m in range(1, count):
                value = value + coeffs[m] * basis[m, f, x]
            (low if x < STEPS else high)[f, x % STEPS] = value
        return carry

    lax.fori_loop(0, fields, field, 0)
    for e, ref in enumerate((base_speed, span_speed, gain)):
        low[fields + e] = ref[:STEPS]
        high[fields + e] = ref[STEPS:]


def edges_kernel(before, low, high, after, packed):
    group = lane_index() // 8

    def field(f, carry):
        value = jnp.zeros((8, LANES), jnp.float32)
        for r in range(4 * STEPS):
            ref = (before, low, high, after)[r // STEPS]
            turned = pltpu.roll(ref[f, r % STEPS], (8 * r + 4) % LANES, 1)
            value = jnp.where(group == r, turned, value)
        packed[f] = value
        return carry

    lax.fori_loop(0, packed.shape[0], field, 0)


def stencil(values, x_up, x_down, z_up, z_down, base, span, gain, mixing, up_wall, down_wall):
    half_x, half_z = 0.5 * base, 0.5 * span
    c_xu, c_xd, c_zu, c_zd = 0.05 - half_x, 0.05 + half_x, 0.05 - half_z, 0.05 + half_z
    out = []
    for f, v in enumerate(values):
        mixed = mixing[f, 0] * values[0]
        for g in range(1, len(values)):
            mixed = mixed + mixing[f, g] * values[g]
        near_x = c_xu * x_up(f) + c_xd * x_down(f)
        near_z = c_zu * z_up(f) + c_zd * z_down(f)
        near_y = up_wall * pltpu.roll(v, 7, 0) + down_wall * pltpu.roll(v, 1, 0)
        out.append((near_x + near_z) + (near_y - 0.3 * v) + gain * mixed)
    return out


def krylov_kernel(
    mixing, before, low, high, after, own, left, right, basis, krylov, sums, state, rim, inject
):
    fields, rows = basis.shape[1], 4 * STEPS
    lane, sub = lane_index(), row_index()
    up_wall = jnp.where(sub < 7, 0.05, 0.0).astype(jnp.float32)
    down_wall = jnp.where(sub > 0, 0.05, 0.0).astype(jnp.float32)
    inner = lane % 8 < 4

    def load(f, carry):
        for q, ref in enumerate((before, low, high, after)):
            for r in range(STEPS):
                state[0, f, q * STEPS + r] = ref[f, r]
        mine = own[f]
        rim[0, f, 0] = jnp.where(inner, left[f], mine)
        rim[0, f, 1] = jnp.where(inner, mine, right[f])
        return carry

    lax.fori_loop(0, fields + EXTRA, load, 0)

    for k in range(STEPS):
        src, dst = state.at[k % 2], state.at[(k + 1) % 2]
        rim_src, rim_dst = rim.at[k % 2], rim.at[(k + 1) % 2]
        for f in range(fields):
            inject[f] = jnp.where(lane % 8 == 5, pltpu.roll(rim_src[f, 0], 2, 1), rim_src[f, 1])
        if k + 1 < STEPS:
            for e in range(2):
                values = [rim_src[f, e] for f in range(fields)]
                made = stencil(
                    values,
                    lambda f: pltpu.roll(values[f], LANES - 8, 1),
                    lambda f: pltpu.roll(values[f], 8, 1),
                    lambda f: pltpu.roll(values[f], LANES - 1, 1),
                    lambda f: pltpu.roll(values[f], 1, 1),
                    rim[0, fields, e],
                    rim[0, fields + 1, e],
                    rim[0, fields + 2, e],
                    mixing,
                    up_wall,
                    down_wall,
                )
                for f in range(fields):
                    rim_dst[f, e] = made[f]

        def row(r, carry):
            values = [src[f, r] for f in range(fields)]
            turned = [pltpu.roll(inject[f], 123 - 8 * r, 1) for f in range(fields)]
            made = stencil(
                values,
                lambda f: src[f, r + 1],
                lambda f: src[f, r - 1],
                lambda f: jnp.where(lane == LANES - 1, turned[f], pltpu.roll(values[f], LANES - 1, 1)),
                lambda f: jnp.where(lane == 0, turned[f], pltpu.roll(values[f], 1, 1)),
                state[0, fields, r],
                state[0, fields + 1, r],
                state[0, fields + 2, r],
                mixing,
                up_wall,
                down_wall,
            )
            for f in range(fields):
                dst[f, r] = made[f]
            return carry

        lax.fori_loop(k + 1, rows - k - 1, row, 0)
        krylov[k] = dst[:fields, STEPS : 3 * STEPS]

    def products(f, totals):
        totals = list(totals)
        for x in range(2 * STEPS):
            new = [krylov[k, f, x] for k in range(STEPS)]
            old = [basis[m, f, x] for m in range(STEPS)]
            i = 0
            for a in range(STEPS):
                for b in range(STEPS):
                    totals[i] = totals[i] + old[a] * new[b]
                    i += 1
            for group in (new, old):
                for a, b in PAIRS:
                    totals[i] = totals[i] + group[a] * group[b]
                    i += 1
        return tuple(totals)

    count = STEPS * STEPS + 2 * len(PAIRS)
    zero = jnp.zeros((8, LANES), jnp.float32)
    totals = lax.fori_loop(0, fields, products, (zero,) * count)
    lines = [jnp.sum(t, axis=0, keepdims=True) for t in totals]
    lines.append(jnp.zeros((LANES - count, LANES), jnp.float32))
    table = jnp.concatenate(lines, axis=0)
    row_sums = lax.dot_general(
        jnp.ones((8, LANES), jnp.float32),
        table,
        (((1,), (1,)), ((), ())),
        precision=lax.Precision.HIGHEST,
        preferred_element_type=jnp.float32,
    )
    for i in range(sums.shape[0]):
        sums[i] = row_sums[0:1]


def finish_kernel(total, parts, krylov, basis, proj_out, factor_out, new_out):
    fields = basis.shape[1]
    line = parts[0]
    for i in range(1, parts.shape[0]):
        line = line + parts[i]
    line = jnp.broadcast_to(line / total, (8, LANES))
    spread = [
        jnp.broadcast_to(line[:, i : i + 1], (8, LANES))
        for i in range(STEPS * STEPS + 2 * len(PAIRS))
    ]
    proj = [[spread[a * STEPS + b] for b in range(STEPS)] for a in range(STEPS)]
    new_new, old_old = {}, {}
    for i, (a, b) in enumerate(PAIRS):
        new_new[a, b] = spread[STEPS * STEPS + i]
        old_old[a, b] = old_old[b, a] = spread[STEPS * STEPS + len(PAIRS) + i]
    turned = [
        [
            sum(old_old[j, i] * proj[i][k] for i in range(STEPS)) - 2.0 * proj[j][k]
            for k in range(STEPS)
        ]
        for j in range(STEPS)
    ]
    gram = {
        (a, b): new_new[a, b] + sum(proj[j][a] * turned[j][b] for j in range(STEPS))
        for a, b in PAIRS
    }
    lower, inverse = {}, []
    for b in range(STEPS):
        for a in range(b, STEPS):
            value = gram[b, a]
            for c in range(b):
                value = value - lower[a, c] * lower[b, c]
            if a == b:
                lower[a, b] = jnp.sqrt(value)
                inverse.append(1.0 / lower[a, b])
            else:
                lower[a, b] = value * inverse[b]
    lane, sub = lane_index(), row_index()
    proj_tile = jnp.zeros((8, LANES), jnp.float32)
    factor_tile = proj_tile
    for a in range(STEPS):
        for b in range(STEPS):
            here = (sub == a) & (lane == b)
            proj_tile = jnp.where(here, proj[a][b], proj_tile)
            if b >= a:
                factor_tile = jnp.where(here, lower[b, a], factor_tile)
    proj_out[...] = proj_tile[:STEPS, :STEPS]
    factor_out[...] = factor_tile[:STEPS, :STEPS]

    def field(f, carry):
        for x in range(2 * STEPS):
            old = [basis[m, f, x] for m in range(STEPS)]
            made = []
            for k in range(STEPS):
                value = krylov[k, f, x]
                for m in range(STEPS):
                    value = value - proj[m][k] * old[m]
                for c in range(k):
                    value = value - lower[k, c] * made[c]
                made.append(value * inverse[k])
                new_out[k, f, x] = made[k]
        return carry

    lax.fori_loop(0, fields, field, 0)


def exchange(value, axes, size):
    up = [(i, (i + 1) % size) for i in range(size)]
    return lambda v: lax.ppermute(v, axes, up), lambda v: lax.ppermute(v, axes, [(j, i) for i, j in up])


def shape_of(*dims):
    return jax.ShapeDtypeStruct(dims, jnp.float32)


def kept(*dims):
    return pltpu.VMEM(dims, jnp.float32)


def near(*arrays):
    return [pltpu.with_memory_space_constraint(a, pltpu.VMEM) for a in arrays]


def on_device(sizes, basis, coeffs, mixing_matrix, base_speed, span_speed, polymer_gain):
    outer, inner, span = sizes
    count, fields, nx, ny, nz = basis.shape
    total = float(basis[0].size * outer * inner * span)
    everything = fields + EXTRA
    slab = kept(everything, STEPS, ny, nz)
    low, high = pl.pallas_call(
        start_kernel,
        out_shape=(slab, slab),
        in_specs=[SMEM, VMEM, VMEM, VMEM, VMEM],
        out_specs=(VMEM, VMEM),
        compiler_params=pltpu.CompilerParams(vmem_limit_bytes=16 * 2**20),
        name="start",
    )(coeffs, *near(basis, base_speed, span_speed, polymer_gain))
    up, down = exchange(low, ("outer", "inner"), outer * inner)
    before, after = up(high), down(low)
    packed = pl.pallas_call(
        edges_kernel,
        out_shape=kept(everything, ny, nz),
        in_specs=[VMEM] * 4,
        out_specs=VMEM,
        compiler_params=pltpu.CompilerParams(vmem_limit_bytes=16 * 2**20),
        name="edges",
    )(*near(before, low, high, after))
    up, down = exchange(packed, "span", span)
    left, right = up(packed), down(packed)
    krylov, sums = pl.pallas_call(
        krylov_kernel,
        out_shape=(kept(STEPS, fields, nx, ny, nz), kept(inner, 1, nz)),
        in_specs=[SMEM] + [VMEM] * 8,
        out_specs=(VMEM, VMEM),
        scratch_shapes=[
            pltpu.VMEM((2, everything, 4 * STEPS, ny, nz), jnp.float32),
            pltpu.VMEM((2, everything, 2, ny, nz), jnp.float32),
            pltpu.VMEM((fields, ny, nz), jnp.float32),
        ],
        compiler_params=pltpu.CompilerParams(vmem_limit_bytes=16 * 2**20),
        name="krylov",
    )(mixing_matrix, *near(before, low, high, after, packed, left, right, basis))
    sums = lax.all_to_all(sums, "inner", 0, 0, tiled=True)
    sums = jnp.broadcast_to(jnp.sum(sums, axis=0, keepdims=True), (outer * span, 1, nz))
    sums = lax.all_to_all(sums, ("outer", "span"), 0, 0, tiled=True)
    return pl.pallas_call(
        functools.partial(finish_kernel, total),
        out_shape=(
            shape_of(count, STEPS),
            shape_of(STEPS, STEPS),
            shape_of(STEPS, fields, nx, ny, nz),
        ),
        in_specs=[VMEM] * 3,
        out_specs=(VMEM, VMEM, VMEM),
        compiler_params=pltpu.CompilerParams(vmem_limit_bytes=16 * 2**20),
        name="finish",
    )(*near(sums, krylov, basis))


def solution(mesh):
    stream, span = mesh.shape["stream"], mesh.shape["span"]
    inner = 1
    while inner * inner < stream * span and stream % (2 * inner) == 0:
        inner *= 2
    outer = stream // inner
    split = Mesh(np.asarray(mesh.devices).reshape(outer, inner, span), ("outer", "inner", "span"))
    field = P(("outer", "inner"), None, "span")
    vectors = P(None, None, ("outer", "inner"), None, "span")
    return jax.shard_map(
        functools.partial(on_device, (outer, inner, span)),
        mesh=split,
        in_specs=(vectors, P(), P(), field, field, field),
        out_specs=(P(), P(), vectors),
        check_vma=False,
    )
```

time: 386 us -> 85.9 us (0.22)
  blocking collectives: 241 us -> 42.5 us
  starting transfers between devices: 73.4 us -> 23.3 us
  matrix products: 30.6 us -> 0 us
  local copies, waits for them, and re-layouts: 22.8 us -> 4.26 us
  Pallas kernels: 0 us -> 10.7 us
  waiting for transfers between devices: 14.4 us -> 3.77 us
    psum x2 -> x0, blocking collectives: 241 us -> none  [the longest x1 123 us: on_device(): proj = lax.psum(local_proj, ('stream', 'span')) / total]
    ppermute x16 -> x4, starting transfers between devices: 73.4 us -> 23.3 us  [the longest x2 14.5 us: exchange(): lax.ppermute(v, axes, [(j, i) for i, j in up])]
    all_to_all x0 -> x2, blocking collectives: none -> 42.5 us  [the longest x1 26.9 us: on_device(): sums = lax.all_to_all(sums, 'inner', 0, 0, tiled=True)]
    dot_general x8 -> x0, matrix products: 27.8 us -> none  [the longest x1 6.78 us: on_device(): jnp.dot(flat_basis, flat_new.T, precision=lax.Precision.HIGHEST)]
    pallas_call x0 -> x4, Pallas kernels: none -> 10.7 us  [the longest x1 7.07 us: on_device(): pl.pallas_call(krylov_kernel, out_shape=(kept(STEPS, fields, nx, ny, nz),...]
    ppermute x16 -> x4, waiting for transfers between devices: 14.4 us -> 3.77 us  [the longest x2 2.71 us: exchange(): lax.ppermute(v, axes, up)]
    ppermute x8 -> x0, local copies, waits for them, and re-layouts: 7.81 us -> none  [the longest x4 3.91 us: padded(): before = lax.ppermute(last, axis, up)]
    slice x20 -> x0, local copies, waits for them, and re-layouts: 7.65 us -> none  [the longest x12 3.41 us: padded(): last = lax.slice_in_dim(value, length - width, length, axis=dim)]
  transfers between devices with their start and end apart: 16 -> 4, of which waited for: 6 -> 2; matrix products, arithmetic and copies ran while one was open for 3% -> 0% of each run, Pallas kernels for 0% -> 0%
where the time goes in v1:
time: 85.9 us; the launch traced here: 85.3 us
  blocking collectives  42.5 us (49%)
  starting transfers between devices  23.3 us (27%)
  Pallas kernels  10.7 us (12%)
  local copies, waits for them, and re-layouts  4.26 us (5%)
  waiting for transfers between devices  3.77 us (4%)
    all_to_all x1, blocking collectives, on_device(): sums = lax.all_to_all(sums, 'inner', 0, 0, tiled=True)  26.9 us
    all_to_all x1, blocking collectives, on_device(): sums = lax.all_to_all(sums, ('outer', 'span'), 0, 0, tiled=True)  15.6 us
    ppermute x2, starting transfers between devices, exchange(): lax.ppermute(v, axes, [(j, i) for i, j in up])  14.5 us
    ppermute x2, starting transfers between devices, exchange(): lax.ppermute(v, axes, up)  8.75 us
    pallas_call x1, Pallas kernels, on_device(): pl.pallas_call(krylov_kernel, out_shape=(kept(STEPS, fields, nx, ny, nz),...  7.07 us
    unnamed x14, local copies, waits for them, and re-layouts  4.24 us
    ppermute x2, waiting for transfers between devices, exchange(): lax.ppermute(v, axes, up)  2.71 us
    pallas_call x1, Pallas kernels, on_device(): pl.pallas_call(functools.partial(finish_kernel, total), out_shape=(shape_...  1.84 us
  transfers between devices with their start and end apart: 4, of which 2 were waited for; matrix products, arithmetic and copies ran while one was open for 0% of the time, Pallas kernels for 0%

profile of v1, /device:TPU:1, one launch (start us, length us, event | category | flops | bytes accessed | tf_op | source)
XLA Modules:
  0.0 85.3 jit_solution(3664360787602091884)
XLA Ops:
  0.6 0.0 copy-start
  0.6 1.3 %copy-done = f32[4,10,8,8,128]{4,3,2,1,0:T(8,128)S(1)} copy-done((f32[4,10,8,8,128]{4,3,2,1,0:T(8,128)S(1)}, f32[4,10,8,8,128]{4,3,2,1,0:T(8,128)}, u32[]{:S(2)}) %copy-start) | copy-done | bytes 1310744
  1.9 0.0 copy-start.2
  2.0 0.8 copy-done.2
  2.7 0.8 copy-done.3
  3.5 0.8 copy-done.4
  4.2 0.7 copy-done.6
  4.9 0.7 start.1
  5.6 5.4 %collective-permute-start = (f32[13,4,8,128]{3,2,1,0:T(8,128)S(1)}, f32[13,4,8,128]{3,2,1,0:T(8,128)S(1)}, u32[]{:S(2)}, u32[]{:S(2)}) collective-permute-start(f32[13,4,8,128]{3,2,1,0:T(8,128)S(1)} %get-tuple-element.7.high), channel_id=1, source_target_pairs={{0,4},{4,8},{8,12},{12,16},{16,20},{20,24},{24,28},{28,32},{32,36}... | collective-permute-start | bytes 638984 | tf_op jit(solution)/shard_map/ppermute | solution.py:243
  11.0 12.6 %collective-permute-start.1 = (f32[13,4,8,128]{3,2,1,0:T(8,128)S(1)}, f32[13,4,8,128]{3,2,1,0:T(8,128)S(1)}, u32[]{:S(2)}, u32[]{:S(2)}) collective-permute-start(f32[13,4,8,128]{3,2,1,0:T(8,128)S(1)} %get-tuple-element.8.low), channel_id=1, source_target_pairs={{4,0},{8,4},{12,8},{16,12},{20,16},{24,20},{28,24},{32,28},{36,32}... | collective-permute-start | bytes 638984 | tf_op jit(solution)/shard_map/ppermute | solution.py:243
  23.6 0.0 collective-permute-done.before
  23.6 1.1 %collective-permute-done.1.after = f32[13,4,8,128]{3,2,1,0:T(8,128)S(1)} collective-permute-done((f32[13,4,8,128]{3,2,1,0:T(8,128)S(1)}, f32[13,4,8,128]{3,2,1,0:T(8,128)S(1)}, u32[]{:S(2)}, u32[]{:S(2)}) %collective-permute-start.1) | collective-permute-done | bytes 213024 | tf_op jit(solution)/shard_map/ppermute | solution.py:243
  24.6 1.1 %edges.1.own = f32[13,8,128]{2,1,0:T(8,128)S(1)} custom-call(f32[13,4,8,128]{3,2,1,0:T(8,128)S(1)} %collective-permute-done.before, f32[13,4,8,128]{3,2,1,0:T(8,128)S(1)} %get-tuple-element.8.low, f32[13,4,8,128]{3,2,1,0:T(8,128)S(1)} %get-tuple-element.7.high, f32[13,4,8,128]{3,2,1,0:T(8,128)S(1)} %collective-permute-done.1.after), custom_call_target="tpu_custom_call" | custom-call | tf_op jit(solution)/shard_map/edges/pallas_call | solution.py:274
  25.8 1.9 %collective-permute-start.3 = (f32[13,8,128]{2,1,0:T(8,128)S(1)}, f32[13,8,128]{2,1,0:T(8,128)S(1)}, u32[]{:S(2)}, u32[]{:S(2)}) collective-permute-start(f32[13,8,128]{2,1,0:T(8,128)S(1)} %edges.1.own), channel_id=1, source_target_pairs={{1,0},{2,1},{3,2},{0,3},{5,4},{6,5},{7,6},{4,7},{9,8},{10,9},{11,1... | collective-permute-start | bytes 159752 | tf_op jit(solution)/shard_map/ppermute | solution.py:243
  27.7 3.4 %collective-permute-start.2 = (f32[13,8,128]{2,1,0:T(8,128)S(1)}, f32[13,8,128]{2,1,0:T(8,128)S(1)}, u32[]{:S(2)}, u32[]{:S(2)}) collective-permute-start(f32[13,8,128]{2,1,0:T(8,128)S(1)} %edges.1.own), channel_id=1, source_target_pairs={{0,1},{1,2},{2,3},{3,0},{4,5},{5,6},{6,7},{7,4},{8,9},{9,10},{10,1... | collective-permute-start | bytes 159752 | tf_op jit(solution)/shard_map/ppermute | solution.py:243
  31.1 0.0 collective-permute-done.3.right
  31.1 2.7 %collective-permute-done.2.left = f32[13,8,128]{2,1,0:T(8,128)S(1)} collective-permute-done((f32[13,8,128]{2,1,0:T(8,128)S(1)}, f32[13,8,128]{2,1,0:T(8,128)S(1)}, u32[]{:S(2)}, u32[]{:S(2)}) %collective-permute-start.2) | collective-permute-done | bytes 53280 | tf_op jit(solution)/shard_map/ppermute | solution.py:243
  33.8 0.0 copy-done.1
  33.8 0.0 copy-done.5
  33.8 7.1 %krylov.1 = (f32[4,10,8,8,128]{4,3,2,1,0:T(8,128)S(1)}, f32[32,1,128]{2,1,0:T(1,128)S(1)}) custom-call(f32[10,10]{1,0:T(8,128)S(1)} %copy-done.5, f32[13,4,8,128]{3,2,1,0:T(8,128)S(1)} %collective-permute-done.before, f32[13,4,8,128]{3,2,1,0:T(8,128)S(1)} %get-tuple-element.8.low, f32[13,4,8,128]{3,2,1,0:T(8,128)S(1)} %get-tuple-element.7.high, ...), custom_call_target="tpu_custom_call" | custom-call | tf_op jit(solution)/shard_map/krylov/pallas_call | solution.py:284
  40.9 26.9 %all_to_all.10 = f32[32,1,128]{2,1,0:T(1,128)S(1)} all-to-all(f32[32,1,128]{2,1,0:T(1,128)S(1)} %get-tuple-element.9), channel_id=1, replica_groups=mesh['outer'=8,'inner'=32,'span'=4] {'inner'}, dimensions={0} | all-to-all | bytes 32768 | tf_op jit(solution)/shard_map/all_to_all | solution.py:297
  67.8 0.1 reduce_sum.9
  67.9 15.6 %all_to_all.11.parts = f32[32,1,128]{2,1,0:T(1,128)S(1)} all-to-all(f32[32,1,128]{2,1,0:T(1,128)S(1)} %broadcast_in_dim.2), channel_id=1, replica_groups=mesh['outer'=8,'inner'=32,'span'=4] {'outer','span'}, dimensions={0} | all-to-all | bytes 32768 | tf_op jit(solution)/shard_map/all_to_all | solution.py:299
  83.5 1.8 %finish.1 = (f32[4,4]{1,0:T(4,128)}, f32[4,4]{1,0:T(4,128)}, f32[4,10,8,8,128]{4,3,2,1,0:T(8,128)}) custom-call(f32[32,1,128]{2,1,0:T(1,128)S(1)} %all_to_all.11.parts, f32[4,10,8,8,128]{4,3,2,1,0:T(8,128)S(1)} %get-tuple-element.10.krylov, f32[4,10,8,8,128]{4,3,2,1,0:T(8,128)S(1)} %copy-done.1), custom_call_target="tpu_custom_call" | custom-call | tf_op jit(solution)/shard_map/finish/pallas_call | solution.py:300
  (6 shorter events, 0.0 us)
Async XLA Ops:
  0.6 1.3 %copy-start = (f32[4,10,8,8,128]{4,3,2,1,0:T(8,128)S(1)}, f32[4,10,8,8,128]{4,3,2,1,0:T(8,128)}, u32[]{:S(2)}) copy-start(f32[4,10,8,8,128]{4,3,2,1,0:T(8,128)} %basis.5) | copy-start | bytes 3932164
  1.9 0.8 copy-start.2
  2.7 0.8 copy-start.3
  3.5 0.8 copy-start.4
  4.2 0.7 copy-start.6
  4.9 28.9 %copy-start.1 = (f32[4,10,8,8,128]{4,3,2,1,0:T(8,128)S(1)}, f32[4,10,8,8,128]{4,3,2,1,0:T(8,128)}, u32[]{:S(2)}) copy-start(f32[4,10,8,8,128]{4,3,2,1,0:T(8,128)} %basis.5) | copy-start | bytes 3932164
  4.9 28.9 %copy-start.5 = (f32[10,10]{1,0:T(8,128)S(1)}, f32[10,10]{1,0:T(8,128)}, u32[]{:S(2)}) copy-start(f32[10,10]{1,0:T(8,128)} %mixing.1) | copy-start | bytes 1204
  5.6 18.0 %collective-permute-start = (f32[13,4,8,128]{3,2,1,0:T(8,128)S(1)}, f32[13,4,8,128]{3,2,1,0:T(8,128)S(1)}, u32[]{:S(2)}, u32[]{:S(2)}) collective-permute-start(f32[13,4,8,128]{3,2,1,0:T(8,128)S(1)} %get-tuple-element.7.high), channel_id=1, source_target_pairs={{0,4},{4,8},{8,12},{12,16},{16,20},{20,24},{24,28},{28,32},{32,36}... | collective-permute-start | bytes 638984 | tf_op jit(solution)/shard_map/ppermute | solution.py:243
  11.0 13.7 %collective-permute-start.1 = (f32[13,4,8,128]{3,2,1,0:T(8,128)S(1)}, f32[13,4,8,128]{3,2,1,0:T(8,128)S(1)}, u32[]{:S(2)}, u32[]{:S(2)}) collective-permute-start(f32[13,4,8,128]{3,2,1,0:T(8,128)S(1)} %get-tuple-element.8.low), channel_id=1, source_target_pairs={{4,0},{8,4},{12,8},{16,12},{20,16},{24,20},{28,24},{32,28},{36,32}... | collective-permute-start | bytes 638984 | tf_op jit(solution)/shard_map/ppermute | solution.py:243
  25.8 5.3 %collective-permute-start.3 = (f32[13,8,128]{2,1,0:T(8,128)S(1)}, f32[13,8,128]{2,1,0:T(8,128)S(1)}, u32[]{:S(2)}, u32[]{:S(2)}) collective-permute-start(f32[13,8,128]{2,1,0:T(8,128)S(1)} %edges.1.own), channel_id=1, source_target_pairs={{1,0},{2,1},{3,2},{0,3},{5,4},{6,5},{7,6},{4,7},{9,8},{10,9},{11,1... | collective-permute-start | bytes 159752 | tf_op jit(solution)/shard_map/ppermute | solution.py:243
  27.7 6.1 %collective-permute-start.2 = (f32[13,8,128]{2,1,0:T(8,128)S(1)}, f32[13,8,128]{2,1,0:T(8,128)S(1)}, u32[]{:S(2)}, u32[]{:S(2)}) collective-permute-start(f32[13,8,128]{2,1,0:T(8,128)S(1)} %edges.1.own), channel_id=1, source_target_pairs={{0,1},{1,2},{2,3},{3,0},{4,5},{5,6},{6,7},{7,4},{8,9},{9,10},{10,1... | collective-permute-start | bytes 159752 | tf_op jit(solution)/shard_map/ppermute | solution.py:243

commit v2 on v1

v2 whole, which is shorter than its diff:
```python
import functools

import jax
import jax.numpy as jnp
import numpy as np
from jax import lax
from jax.experimental import pallas as pl
from jax.experimental.pallas import tpu as pltpu
from jax.sharding import Mesh
from jax.sharding import PartitionSpec as P

STEPS = 4
LANES = 128
EXTRA = 3
VMEM = pl.BlockSpec(memory_space=pltpu.VMEM)
SMEM = pl.BlockSpec(memory_space=pltpu.SMEM)
HBM = pl.BlockSpec(memory_space=pltpu.HBM)
PAIRS = [(a, b) for a in range(STEPS) for b in range(a, STEPS)]


def lane_index():
    return lax.broadcasted_iota(jnp.int32, (8, LANES), 1)


def row_index():
    return lax.broadcasted_iota(jnp.int32, (8, LANES), 0)


def start_kernel(coeffs, basis, base_speed, span_speed, gain, low, high, held, weights, weight_sem, basis_sems, field_sems):
    count, fields = basis.shape[0], basis.shape[1]
    weight_copy = pltpu.make_async_copy(coeffs, weights, weight_sem)
    weight_copy.start()

    def basis_copy(f):
        return pltpu.make_async_copy(basis.at[:, f], held.at[:, f], basis_sems.at[f])

    for f in range(fields):
        basis_copy(f).start()
    copies = []
    for e, ref in enumerate((base_speed, span_speed, gain)):
        for part, out in enumerate((low, high)):
            copies.append(
                pltpu.make_async_copy(
                    ref.at[pl.ds(part * STEPS, STEPS)], out.at[fields + e], field_sems.at[e, part]
                )
            )
            copies[-1].start()
    weight_copy.wait()
    scale = [weights[m] for m in range(count)]

    def field(f, carry):
        basis_copy(f).wait()
        for x in range(2 * STEPS):
            value = scale[0] * held[0, f, x]
            for m in range(1, count):
                value = value + scale[m] * held[m, f, x]
            (low if x < STEPS else high)[f, x % STEPS] = value
        return carry

    lax.fori_loop(0, fields, field, 0)
    for copy in copies:
        copy.wait()


def pack(tiles, value):
    group = lane_index() // 8
    for r, tile in tiles:
        turned = pltpu.roll(tile, (8 * r + 4) % LANES, 1)
        value = jnp.where(group == r, turned, value)
    return value


def prepare_kernel(mixing, low, high, held, own, old_sums, splat):
    fields = held.shape[1]
    for f in range(fields):
        for g in range(fields):
            splat[f * fields + g] = jnp.full((8, LANES), mixing[f, g], jnp.float32)
    blank = jnp.zeros((8, LANES), jnp.float32)

    def field(f, carry):
        rows = [(STEPS + r, low[f, r]) for r in range(STEPS)]
        rows += [(2 * STEPS + r, high[f, r]) for r in range(STEPS)]
        own[f] = pack(rows, blank)
        return carry

    lax.fori_loop(0, own.shape[0], field, 0)

    def products(f, totals):
        totals = list(totals)
        for x in range(2 * STEPS):
            old = [held[m, f, x] for m in range(STEPS)]
            for i, (a, b) in enumerate(PAIRS):
                totals[i] = totals[i] + old[a] * old[b]
        return tuple(totals)

    totals = lax.fori_loop(0, fields, products, (blank,) * len(PAIRS))
    for i, total in enumerate(totals):
        old_sums[i] = total


def edges_kernel(before, after, own, packed):
    def field(f, carry):
        rows = [(r, before[f, r]) for r in range(STEPS)]
        rows += [(3 * STEPS + r, after[f, r]) for r in range(STEPS)]
        packed[f] = pack(rows, own[f])
        return carry

    lax.fori_loop(0, own.shape[0], field, 0)


def speeds(base, span):
    half_x, half_z = 0.5 * base, 0.5 * span
    return 0.05 - half_x, 0.05 + half_x, 0.05 - half_z, 0.05 + half_z


def walls():
    sub = row_index()
    return (
        jnp.where(sub < 7, 0.05, 0.0).astype(jnp.float32),
        jnp.where(sub > 0, 0.05, 0.0).astype(jnp.float32),
    )


def stencil(splat, items, wall, store):
    fields = len(items[0][0])
    scales = [speeds(item[5], item[6]) for item in items]
    for f in range(fields):
        mixed = [None] * len(items)
        for g in range(fields):
            weight = splat[f * fields + g]
            for i, item in enumerate(items):
                part = weight * item[0][g]
                mixed[i] = part if g == 0 else mixed[i] + part
        for i, (values, x_up, x_down, z_up, z_down, _, _, gain) in enumerate(items):
            c_xu, c_xd, c_zu, c_zd = scales[i]
            v = values[f]
            near_x = c_xu * x_up(f) + c_xd * x_down(f)
            near_z = c_zu * z_up(f) + c_zd * z_down(f)
            near_y = wall[0] * pltpu.roll(v, 7, 0) + wall[1] * pltpu.roll(v, 1, 0)
            store(i, f, (near_x + near_z) + (near_y - 0.3 * v) + gain * mixed[i])


def first_kernel(splat, before, low, high, after, made, coefs):
    fields, rows = before.shape[0] - EXTRA, 4 * STEPS
    parts = (before, low, high, after)
    lane, wall = lane_index(), walls()
    for e in range(EXTRA):
        for r in range(rows):
            coefs[e, r] = parts[r // STEPS][fields + e, r % STEPS]

    def tile(f, r):
        return parts[r // STEPS][f, r % STEPS]

    def item(r):
        values = [tile(f, r) for f in range(fields)]
        return (
            values,
            lambda f: tile(f, r + 1),
            lambda f: tile(f, r - 1),
            lambda f: jnp.where(lane == LANES - 1, 0.0, pltpu.roll(values[f], LANES - 1, 1)),
            lambda f: jnp.where(lane == 0, 0.0, pltpu.roll(values[f], 1, 1)),
            tile(fields, r),
            tile(fields + 1, r),
            tile(fields + 2, r),
        )

    for r in range(1, rows - 1, 2):

        def store(i, f, value, r=r):
            made[f, r + i] = value

        stencil(splat, [item(r), item(r + 1)], wall, store)


def krylov_kernel(
    splat, own, left, right, made, coefs, held, old_sums, krylov, sums, state, rim, inject
):
    fields, rows = held.shape[1], 4 * STEPS
    lane, wall = lane_index(), walls()
    inner = lane % 8 < 4

    def load(f, carry):
        mine = own[f]
        rim[0, f, 0] = jnp.where(inner, left[f], mine)
        rim[0, f, 1] = jnp.where(inner, mine, right[f])
        return carry

    lax.fori_loop(0, fields + EXTRA, load, 0)

    for k in range(STEPS):
        src = state.at[k % 2]
        dst = state.at[(k + 1) % 2]
        rim_src, rim_dst = rim.at[k % 2], rim.at[(k + 1) % 2]
        for f in range(fields):
            inject[f] = jnp.where(lane % 8 == 5, pltpu.roll(rim_src[f, 0], 2, 1), rim_src[f, 1])
        if k + 1 < STEPS:

            def edge(e):
                values = [rim_src[f, e] for f in range(fields)]
                return (
                    values,
                    lambda f: pltpu.roll(values[f], LANES - 8, 1),
                    lambda f: pltpu.roll(values[f], 8, 1),
                    lambda f: pltpu.roll(values[f], LANES - 1, 1),
                    lambda f: pltpu.roll(values[f], 1, 1),
                    rim[0, fields, e],
                    rim[0, fields + 1, e],
                    rim[0, fields + 2, e],
                )

            def edge_store(i, f, value):
                rim_dst[f, i] = value

            stencil(splat, [edge(0), edge(1)], wall, edge_store)

        def turned(f, r):
            return pltpu.roll(inject[f], 123 - 8 * r, 1)

        if k == 0:

            def fix(r, carry):
                _, _, c_zu, c_zd = speeds(coefs[0, r], coefs[1, r])
                scale = jnp.where(lane == LANES - 1, c_zu, jnp.where(lane == 0, c_zd, 0.0))
                for f in range(fields):
                    dst[f, r] = made[f, r] + scale * turned(f, r)
                return carry

            lax.fori_loop(1, rows - 1, fix, 0)
            krylov[0] = dst[:, STEPS : 3 * STEPS]
            continue

        def item(r):
            values = [src[f, r] for f in range(fields)]
            return (
                values,
                lambda f: src[f, r + 1],
                lambda f: src[f, r - 1],
                lambda f: jnp.where(
                    lane == LANES - 1, turned(f, r), pltpu.roll(values[f], LANES - 1, 1)
                ),
                lambda f: jnp.where(lane == 0, turned(f, r), pltpu.roll(values[f], 1, 1)),
                coefs[0, r],
                coefs[1, r],
                coefs[2, r],
            )

        def row(q, carry):
            r = k + 1 + 2 * q

            def store(i, f, value):
                dst[f, r + i] = value

            stencil(splat, [item(r), item(r + 1)], wall, store)
            return carry

        lax.fori_loop(0, (rows - 2 * k - 2) // 2, row, 0)
        krylov[k] = dst[:, STEPS : 3 * STEPS]

    def products(f, totals):
        totals = list(totals)
        for x in range(2 * STEPS):
            new = [krylov[k, f, x] for k in range(STEPS)]
            old = [held[m, f, x] for m in range(STEPS)]
            i = 0
            for a in range(STEPS):
                for b in range(STEPS):
                    totals[i] = totals[i] + old[a] * new[b]
                    i += 1
            for a, b in PAIRS:
                totals[i] = totals[i] + new[a] * new[b]
                i += 1
        return tuple(totals)

    zero = jnp.zeros((8, LANES), jnp.float32)
    totals = lax.fori_loop(0, fields, products, (zero,) * (STEPS * STEPS + len(PAIRS)))
    totals = list(totals) + [old_sums[i] for i in range(len(PAIRS))]
    lines = [jnp.sum(t, axis=0, keepdims=True) for t in totals]
    lines.append(jnp.zeros((LANES - len(lines), LANES), jnp.float32))
    table = jnp.concatenate(lines, axis=0)
    row_sums = lax.dot_general(
        jnp.ones((8, LANES), jnp.float32),
        table,
        (((1,), (1,)), ((), ())),
        precision=lax.Precision.HIGHEST,
        preferred_element_type=jnp.float32,
    )
    for i in range(sums.shape[0]):
        sums[i] = row_sums[0:1]


def finish_kernel(total, parts, krylov, basis, proj_out, factor_out, new_out, buffer, sems):
    fields = basis.shape[1]
    line = parts[0]
    for i in range(1, parts.shape[0]):
        line = line + parts[i]
    line = jnp.broadcast_to(line / total, (8, LANES))
    spread = [
        jnp.broadcast_to(line[:, i : i + 1], (8, LANES))
        for i in range(STEPS * STEPS + 2 * len(PAIRS))
    ]
    proj = [[spread[a * STEPS + b] for b in range(STEPS)] for a in range(STEPS)]
    new_new, old_old = {}, {}
    for i, (a, b) in enumerate(PAIRS):
        new_new[a, b] = spread[STEPS * STEPS + i]
        old_old[a, b] = old_old[b, a] = spread[STEPS * STEPS + len(PAIRS) + i]
    turned = [
        [
            sum(old_old[j, i] * proj[i][k] for i in range(STEPS)) - 2.0 * proj[j][k]
            for k in range(STEPS)
        ]
        for j in range(STEPS)
    ]
    gram = {
        (a, b): new_new[a, b] + sum(proj[j][a] * turned[j][b] for j in range(STEPS))
        for a, b in PAIRS
    }
    lower, inverse = {}, []
    for b in range(STEPS):
        for a in range(b, STEPS):
            value = gram[b, a]
            for c in range(b):
                value = value - lower[a, c] * lower[b, c]
            if a == b:
                lower[a, b] = jnp.sqrt(value)
                inverse.append(1.0 / lower[a, b])
            else:
                lower[a, b] = value * inverse[b]
    lane, sub = lane_index(), row_index()
    proj_tile = jnp.zeros((8, LANES), jnp.float32)
    factor_tile = proj_tile
    for a in range(STEPS):
        for b in range(STEPS):
            here = (sub == a) & (lane == b)
            proj_tile = jnp.where(here, proj[a][b], proj_tile)
            if b >= a:
                factor_tile = jnp.where(here, lower[b, a], factor_tile)
    proj_out[...] = proj_tile[:STEPS, :STEPS]
    factor_out[...] = factor_tile[:STEPS, :STEPS]

    def field(f, carry):
        for x in range(2 * STEPS):
            old = [basis[m, f, x] for m in range(STEPS)]
            made = []
            for k in range(STEPS):
                value = krylov[k, f, x]
                for m in range(STEPS):
                    value = value - proj[m][k] * old[m]
                for c in range(k):
                    value = value - lower[k, c] * made[c]
                made.append(value * inverse[k])
                buffer[k, f, x] = made[k]
        out_copy(f).start()
        return carry

    def out_copy(f):
        return pltpu.make_async_copy(buffer.at[:, f], new_out.at[:, f], sems.at[f])

    lax.fori_loop(0, fields, field, 0)
    for f in range(fields):
        out_copy(f).wait()


def far(*arrays):
    return [pltpu.with_memory_space_constraint(a, pltpu.HBM) for a in arrays]


def ring(axes, size):
    up = [(i, (i + 1) % size) for i in range(size)]
    down = [(j, i) for i, j in up]
    return lambda v: lax.ppermute(v, axes, up), lambda v: lax.ppermute(v, axes, down)


def shape_of(*dims):
    return jax.ShapeDtypeStruct(dims, jnp.float32)


def kept(*dims):
    return pltpu.VMEM(dims, jnp.float32)


def near(*arrays):
    return [pltpu.with_memory_space_constraint(a, pltpu.VMEM) for a in arrays]


def on_device(sizes, basis, coeffs, mixing_matrix, base_speed, span_speed, polymer_gain):
    outer, inner, span = sizes
    count, fields, nx, ny, nz = basis.shape
    total = float(basis[0].size * outer * inner * span)
    everything = fields + EXTRA
    slab = kept(everything, STEPS, ny, nz)
    vectors = (count, fields, nx, ny, nz)
    params = pltpu.CompilerParams(vmem_limit_bytes=16 * 2**20)
    low, high, held = pl.pallas_call(
        start_kernel,
        out_shape=(slab, slab, kept(*vectors)),
        in_specs=[HBM] * 5,
        out_specs=(VMEM,) * 3,
        scratch_shapes=[
            pltpu.SMEM((count,), jnp.float32),
            pltpu.SemaphoreType.DMA(()),
            pltpu.SemaphoreType.DMA((fields,)),
            pltpu.SemaphoreType.DMA((EXTRA, 2)),
        ],
        compiler_params=params,
        name="start",
    )(*far(coeffs, basis, base_speed, span_speed, polymer_gain))
    up, down = ring(("outer", "inner"), outer * inner)
    before, after = up(high), down(low)
    own, old_sums, splat = pl.pallas_call(
        prepare_kernel,
        out_shape=(
            kept(everything, ny, nz),
            kept(len(PAIRS), ny, nz),
            kept(fields * fields, ny, nz),
        ),
        in_specs=[SMEM] + [VMEM] * 3,
        out_specs=(VMEM,) * 3,
        compiler_params=params,
        name="prepare",
    )(mixing_matrix, *near(low, high, held))
    packed = pl.pallas_call(
        edges_kernel,
        out_shape=kept(everything, ny, nz),
        in_specs=[VMEM] * 3,
        out_specs=VMEM,
        compiler_params=params,
        name="edges",
    )(*near(before, after, own))
    up, down = ring("span", span)
    left, right = up(packed), down(packed)
    made, coefs = pl.pallas_call(
        first_kernel,
        out_shape=(kept(fields, 4 * STEPS, ny, nz), kept(EXTRA, 4 * STEPS, ny, nz)),
        in_specs=[VMEM] * 5,
        out_specs=(VMEM,) * 2,
        compiler_params=params,
        name="first",
    )(*near(splat, before, low, high, after))
    krylov, sums = pl.pallas_call(
        krylov_kernel,
        out_shape=(kept(*vectors), kept(inner, 1, nz)),
        in_specs=[VMEM] * 8,
        out_specs=(VMEM,) * 2,
        scratch_shapes=[
            pltpu.VMEM((2, fields, 4 * STEPS, ny, nz), jnp.float32),
            pltpu.VMEM((2, everything, 2, ny, nz), jnp.float32),
            pltpu.VMEM((fields, ny, nz), jnp.float32),
        ],
        compiler_params=params,
        name="krylov",
    )(*near(splat, packed, left, right, made, coefs, held, old_sums))
    sums = lax.all_to_all(sums, "inner", 0, 0, tiled=True)
    sums = jnp.broadcast_to(jnp.sum(sums, axis=0, keepdims=True), (outer * span, 1, nz))
    sums = lax.all_to_all(sums, ("outer", "span"), 0, 0, tiled=True)
    return pl.pallas_call(
        functools.partial(finish_kernel, total),
        out_shape=(shape_of(count, STEPS), shape_of(STEPS, STEPS), shape_of(*vectors)),
        in_specs=[VMEM] * 3,
        out_specs=(VMEM, VMEM, HBM),
        scratch_shapes=[
            pltpu.VMEM(vectors, jnp.float32),
            pltpu.SemaphoreType.DMA((fields,)),
        ],
        compiler_params=params,
        name="finish",
    )(*near(sums, krylov, held))


def solution(mesh):
    stream, span = mesh.shape["stream"], mesh.shape["span"]
    inner = 1
    while inner * inner < stream * span and stream % (2 * inner) == 0:
        inner *= 2
    outer = stream // inner
    split = Mesh(np.asarray(mesh.devices).reshape(outer, inner, span), ("outer", "inner", "span"))
    field = P(("outer", "inner"), None, "span")
    vectors = P(None, None, ("outer", "inner"), None, "span")
    return jax.shard_map(
        functools.partial(on_device, (outer, inner, span)),
        mesh=split,
        in_specs=(vectors, P(), P(), field, field, field),
        out_specs=(P(), P(), vectors),
        check_vma=False,
    )
```

time: 85.9 us -> 82.1 us (0.956)
  blocking collectives: 42.5 us -> 36.1 us
  waiting for transfers between devices: 3.77 us -> 8.34 us
  local copies, waits for them, and re-layouts: 4.26 us -> 0.02 us
  Pallas kernels: 10.7 us -> 12.2 us
  starting transfers between devices: 23.3 us -> 24.3 us
    ppermute x4, waiting for transfers between devices: 3.77 us -> 8.34 us  [the longest x2 8.34 us: ring(): lax.ppermute(v, axes, up)]
    unnamed x14 -> x2, local copies, waits for them, and re-layouts: 4.24 us -> 0.01 us
    all_to_all x1, blocking collectives: 26.9 us -> 23.6 us  [on_device(): sums = lax.all_to_all(sums, 'inner', 0, 0, tiled=True)]
    all_to_all x1, blocking collectives: 15.6 us -> 12.6 us  [on_device(): sums = lax.all_to_all(sums, ('outer', 'span'), 0, 0, tiled=True)]
    pallas_call x2 -> x4, Pallas kernels: 7.76 us -> 9.11 us  [the longest x1 4.8 us: on_device(): pl.pallas_call(krylov_kernel, out_shape=(kept(*vectors), kept(inner, 1, n...]
    ppermute x4, starting transfers between devices: 23.3 us -> 24.3 us  [the longest x2 20.4 us: ring(): lax.ppermute(v, axes, down)]
  transfers between devices with their start and end apart: 4 -> 4, of which waited for: 2 -> 2; matrix products, arithmetic and copies ran while one was open for 0% -> 0% of each run, Pallas kernels for 0% -> 3%
where the time goes in v2:
time: 82.1 us; the launch traced here: 81.8 us
  blocking collectives  36.1 us (44%)
  starting transfers between devices  24.3 us (30%)
  Pallas kernels  12.2 us (15%)
  waiting for transfers between devices  8.34 us (10%)
    all_to_all x1, blocking collectives, on_device(): sums = lax.all_to_all(sums, 'inner', 0, 0, tiled=True)  23.6 us
    ppermute x2, starting transfers between devices, ring(): lax.ppermute(v, axes, down)  20.4 us
    all_to_all x1, blocking collectives, on_device(): sums = lax.all_to_all(sums, ('outer', 'span'), 0, 0, tiled=True)  12.6 us
    ppermute x2, waiting for transfers between devices, ring(): lax.ppermute(v, axes, up)  8.34 us
    pallas_call x1, Pallas kernels, on_device(): pl.pallas_call(krylov_kernel, out_shape=(kept(*vectors), kept(inner, 1, n...  4.8 us
    ppermute x2, starting transfers between devices, ring(): lax.ppermute(v, axes, up)  3.84 us
    pallas_call x1, Pallas kernels, on_device(): pl.pallas_call(functools.partial(finish_kernel, total), out_shape=(shape_...  2.11 us
    pallas_call x1, Pallas kernels, on_device(): pl.pallas_call(prepare_kernel, out_shape=(kept(everything, ny, nz), kept(...  1.94 us
  transfers between devices with their start and end apart: 4, of which 2 were waited for; matrix products, arithmetic and copies ran while one was open for 0% of the time, Pallas kernels for 3%

profile of v2, /device:TPU:1, one launch (start us, length us, event | category | flops | bytes accessed | tf_op | source)
XLA Modules:
  0.0 81.8 jit_solution(15079204995379386318)
XLA Ops:
  0.6 0.0 copy-start
  0.6 1.6 %start.1 = (f32[13,4,8,128]{3,2,1,0:T(8,128)S(1)}, f32[13,4,8,128]{3,2,1,0:T(8,128)S(1)}, f32[4,10,8,8,128]{4,3,2,1,0:T(8,128)S(1)}) custom-call(f32[4]{0:T(128)} %coeffs.1, f32[4,10,8,8,128]{4,3,2,1,0:T(8,128)} %basis.1, f32[8,8,128]{2,1,0:T(8,128)} %base_speed.1, f32[8,8,128]{2,1,0:T(8,128)} %span_speed.1, f32[8,8,128]{2,1,0:T(8,128)} %gain.1), custom_call_target="tpu_custom_call" | custom-call | tf_op jit(solution)/shard_map/start/pallas_call | solution.py:393
  2.2 16.1 %collective-permute-start.1 = (f32[13,4,8,128]{3,2,1,0:T(8,128)S(1)}, f32[13,4,8,128]{3,2,1,0:T(8,128)S(1)}, u32[]{:S(2)}, u32[]{:S(2)}) collective-permute-start(f32[13,4,8,128]{3,2,1,0:T(8,128)S(1)} %get-tuple-element.13.low), channel_id=1, source_target_pairs={{4,0},{8,4},{12,8},{16,12},{20,16},{24,20},{28,24},{32,28},{36,32}... | collective-permute-start | bytes 638984 | tf_op jit(solution)/shard_map/ppermute | solution.py:370
  18.3 1.9 %collective-permute-start = (f32[13,4,8,128]{3,2,1,0:T(8,128)S(1)}, f32[13,4,8,128]{3,2,1,0:T(8,128)S(1)}, u32[]{:S(2)}, u32[]{:S(2)}) collective-permute-start(f32[13,4,8,128]{3,2,1,0:T(8,128)S(1)} %get-tuple-element.14.high), channel_id=1, source_target_pairs={{0,4},{4,8},{8,12},{12,16},{16,20},{20,24},{24,28},{28,32},{32,36}... | collective-permute-start | bytes 638984 | tf_op jit(solution)/shard_map/ppermute | solution.py:370
  20.2 0.0 copy-done
  20.2 1.9 %prepare.1 = (f32[13,8,128]{2,1,0:T(8,128)S(1)}, f32[10,8,128]{2,1,0:T(8,128)S(1)}, f32[100,8,128]{2,1,0:T(8,128)S(1)}) custom-call(f32[10,10]{1,0:T(8,128)S(1)} %copy-done, f32[13,4,8,128]{3,2,1,0:T(8,128)S(1)} %get-tuple-element.13.low, f32[13,4,8,128]{3,2,1,0:T(8,128)S(1)} %get-tuple-element.14.high, f32[4,10,8,8,128]{4,3,2,1,0:T(8,128)S(1)} %get-tuple-element.15.held.basis), custom_call_target="tpu_custom_call" | custom-call | tf_op jit(solution)/shard_map/prepare/pallas_call | solution.py:409
  22.2 0.0 collective-permute-done.1.after
  22.2 5.0 %collective-permute-done.before = f32[13,4,8,128]{3,2,1,0:T(8,128)S(1)} collective-permute-done((f32[13,4,8,128]{3,2,1,0:T(8,128)S(1)}, f32[13,4,8,128]{3,2,1,0:T(8,128)S(1)}, u32[]{:S(2)}, u32[]{:S(2)}) %collective-permute-start) | collective-permute-done | bytes 213024 | tf_op jit(solution)/shard_map/ppermute | solution.py:370
  27.2 1.0 %edges.1.own = f32[13,8,128]{2,1,0:T(8,128)S(1)} custom-call(f32[13,4,8,128]{3,2,1,0:T(8,128)S(1)} %collective-permute-done.before, f32[13,4,8,128]{3,2,1,0:T(8,128)S(1)} %collective-permute-done.1.after, f32[13,8,128]{2,1,0:T(8,128)S(1)} %get-tuple-element.17.own), custom_call_target="tpu_custom_call" | custom-call | tf_op jit(solution)/shard_map/edges/pallas_call | solution.py:421
  28.2 4.4 %collective-permute-start.3 = (f32[13,8,128]{2,1,0:T(8,128)S(1)}, f32[13,8,128]{2,1,0:T(8,128)S(1)}, u32[]{:S(2)}, u32[]{:S(2)}) collective-permute-start(f32[13,8,128]{2,1,0:T(8,128)S(1)} %edges.1.own), channel_id=1, source_target_pairs={{1,0},{2,1},{3,2},{0,3},{5,4},{6,5},{7,6},{4,7},{9,8},{10,9},{11,1... | collective-permute-start | bytes 159752 | tf_op jit(solution)/shard_map/ppermute | solution.py:370
  32.6 1.9 %collective-permute-start.2 = (f32[13,8,128]{2,1,0:T(8,128)S(1)}, f32[13,8,128]{2,1,0:T(8,128)S(1)}, u32[]{:S(2)}, u32[]{:S(2)}) collective-permute-start(f32[13,8,128]{2,1,0:T(8,128)S(1)} %edges.1.own), channel_id=1, source_target_pairs={{0,1},{1,2},{2,3},{3,0},{4,5},{5,6},{6,7},{7,4},{8,9},{9,10},{10,1... | collective-permute-start | bytes 159752 | tf_op jit(solution)/shard_map/ppermute | solution.py:370
  34.5 0.8 first.1
  35.3 0.0 collective-permute-done.3.right
  35.3 3.4 %collective-permute-done.2.left = f32[13,8,128]{2,1,0:T(8,128)S(1)} collective-permute-done((f32[13,8,128]{2,1,0:T(8,128)S(1)}, f32[13,8,128]{2,1,0:T(8,128)S(1)}, u32[]{:S(2)}, u32[]{:S(2)}) %collective-permute-start.2) | collective-permute-done | bytes 53280 | tf_op jit(solution)/shard_map/ppermute | solution.py:370
  38.7 4.8 %krylov.1 = (f32[4,10,8,8,128]{4,3,2,1,0:T(8,128)S(1)}, f32[32,1,128]{2,1,0:T(1,128)S(1)}) custom-call(f32[100,8,128]{2,1,0:T(8,128)S(1)} %get-tuple-element.16.splat, f32[13,8,128]{2,1,0:T(8,128)S(1)} %edges.1.own, f32[13,8,128]{2,1,0:T(8,128)S(1)} %collective-permute-done.2.left, f32[13,8,128]{2,1,0:T(8,128)S(1)} %collective-permute-done.3.right, ...), custom_call_target="tpu_custom_call" | custom-call | tf_op jit(solution)/shard_map/krylov/pallas_call | solution.py:439
  43.5 23.6 %all_to_all.10 = f32[32,1,128]{2,1,0:T(1,128)S(1)} all-to-all(f32[32,1,128]{2,1,0:T(1,128)S(1)} %get-tuple-element.21), channel_id=1, replica_groups=mesh['outer'=8,'inner'=32,'span'=4] {'inner'}, dimensions={0} | all-to-all | bytes 32768 | tf_op jit(solution)/shard_map/all_to_all | solution.py:452
  67.0 0.1 reduce_sum.9
  67.1 12.6 %all_to_all.11.parts = f32[32,1,128]{2,1,0:T(1,128)S(1)} all-to-all(f32[32,1,128]{2,1,0:T(1,128)S(1)} %broadcast_in_dim.2), channel_id=1, replica_groups=mesh['outer'=8,'inner'=32,'span'=4] {'outer','span'}, dimensions={0} | all-to-all | bytes 32768 | tf_op jit(solution)/shard_map/all_to_all | solution.py:454
  79.7 2.1 %finish.1 = (f32[4,4]{1,0:T(4,128)}, f32[4,4]{1,0:T(4,128)}, f32[4,10,8,8,128]{4,3,2,1,0:T(8,128)}) custom-call(f32[32,1,128]{2,1,0:T(1,128)S(1)} %all_to_all.11.parts, f32[4,10,8,8,128]{4,3,2,1,0:T(8,128)S(1)} %get-tuple-element.22.krylov, f32[4,10,8,8,128]{4,3,2,1,0:T(8,128)S(1)} %get-tuple-element.15.held.basis), custom_call_target="tpu_custom_call" | custom-call | tf_op jit(solution)/shard_map/finish/pallas_call | solution.py:455
  (1 shorter events, 0.0 us)
Async XLA Ops:
  0.6 19.6 %copy-start = (f32[10,10]{1,0:T(8,128)S(1)}, f32[10,10]{1,0:T(8,128)}, u32[]{:S(2)}) copy-start(f32[10,10]{1,0:T(8,128)} %mixing.1) | copy-start | bytes 1204
  2.2 20.0 %collective-permute-start.1 = (f32[13,4,8,128]{3,2,1,0:T(8,128)S(1)}, f32[13,4,8,128]{3,2,1,0:T(8,128)S(1)}, u32[]{:S(2)}, u32[]{:S(2)}) collective-permute-start(f32[13,4,8,128]{3,2,1,0:T(8,128)S(1)} %get-tuple-element.13.low), channel_id=1, source_target_pairs={{4,0},{8,4},{12,8},{16,12},{20,16},{24,20},{28,24},{32,28},{36,32}... | collective-permute-start | bytes 638984 | tf_op jit(solution)/shard_map/ppermute | solution.py:370
  18.3 8.9 %collective-permute-start = (f32[13,4,8,128]{3,2,1,0:T(8,128)S(1)}, f32[13,4,8,128]{3,2,1,0:T(8,128)S(1)}, u32[]{:S(2)}, u32[]{:S(2)}) collective-permute-start(f32[13,4,8,128]{3,2,1,0:T(8,128)S(1)} %get-tuple-element.14.high), channel_id=1, source_target_pairs={{0,4},{4,8},{8,12},{12,16},{16,20},{20,24},{24,28},{28,32},{32,36}... | collective-permute-start | bytes 638984 | tf_op jit(solution)/shard_map/ppermute | solution.py:370
  28.2 7.1 %collective-permute-start.3 = (f32[13,8,128]{2,1,0:T(8,128)S(1)}, f32[13,8,128]{2,1,0:T(8,128)S(1)}, u32[]{:S(2)}, u32[]{:S(2)}) collective-permute-start(f32[13,8,128]{2,1,0:T(8,128)S(1)} %edges.1.own), channel_id=1, source_target_pairs={{1,0},{2,1},{3,2},{0,3},{5,4},{6,5},{7,6},{4,7},{9,8},{10,9},{11,1... | collective-permute-start | bytes 159752 | tf_op jit(solution)/shard_map/ppermute | solution.py:370
  32.6 6.1 %collective-permute-start.2 = (f32[13,8,128]{2,1,0:T(8,128)S(1)}, f32[13,8,128]{2,1,0:T(8,128)S(1)}, u32[]{:S(2)}, u32[]{:S(2)}) collective-permute-start(f32[13,8,128]{2,1,0:T(8,128)S(1)} %edges.1.own), channel_id=1, source_target_pairs={{0,1},{1,2},{2,3},{3,0},{4,5},{5,6},{6,7},{7,4},{8,9},{9,10},{10,1... | collective-permute-start | bytes 159752 | tf_op jit(solution)/shard_map/ppermute | solution.py:370

commit v3 on v2

--- a/solution.py
+++ b/solution.py
@@ -26,22 +26,36 @@
     return lax.broadcasted_iota(jnp.int32, (8, LANES), 0)
 
 
-def start_kernel(coeffs, basis, base_speed, span_speed, gain, low, high, held, weights, weight_sem, basis_sems, field_sems):
+def parity():
+    return lax.axis_index("inner") % 2
+
+
+def start_kernel(
+    coeffs, basis, base_speed, span_speed, gain, cross, chip, held, weights, weight_sem, basis_sems, field_sems
+):
     count, fields = basis.shape[0], basis.shape[1]
+    half = fields // 2
+    first_row = STEPS * parity()
+    sides = ((cross, first_row), (chip, STEPS - first_row))
     weight_copy = pltpu.make_async_copy(coeffs, weights, weight_sem)
     weight_copy.start()
-
-    def basis_copy(f):
-        return pltpu.make_async_copy(basis.at[:, f], held.at[:, f], basis_sems.at[f])
-
-    for f in range(fields):
-        basis_copy(f).start()
+    waves = []
+    for w in range(2):
+        span = pl.ds(w * half, half)
+        waves.append(
+            [
+                pltpu.make_async_copy(basis.at[m, span], held.at[m, span], basis_sems.at[w, m])
+                for m in range(count)
+            ]
+        )
+        for copy in waves[w]:
+            copy.start()
     copies = []
     for e, ref in enumerate((base_speed, span_speed, gain)):
-        for part, out in enumerate((low, high)):
+        for i, (out, row) in enumerate(sides):
             copies.append(
                 pltpu.make_async_copy(
-                    ref.at[pl.ds(part * STEPS, STEPS)], out.at[fields + e], field_sems.at[e, part]
+                    ref.at[pl.ds(row, STEPS)], out.at[fields + e], field_sems.at[e, i]
                 )
             )
             copies[-1].start()
@@ -49,15 +63,18 @@
     scale = [weights[m] for m in range(count)]
 
     def field(f, carry):
-        basis_copy(f).wait()
-        for x in range(2 * STEPS):
-            value = scale[0] * held[0, f, x]
-            for m in range(1, count):
-                value = value + scale[m] * held[m, f, x]
-            (low if x < STEPS else high)[f, x % STEPS] = value
+        for r in range(STEPS):
+            for out, row in sides:
+                value = scale[0] * held[0, f, row + r]
+                for m in range(1, count):
+                    value = value + scale[m] * held[m, f, row + r]
+                out[f, r] = value
         return carry
 
-    lax.fori_loop(0, fields, field, 0)
+    for w in range(2):
+        for copy in waves[w]:
+            copy.wait()
+        lax.fori_loop(w * half, (w + 1) * half, field, 0)
     for copy in copies:
         copy.wait()
 
@@ -65,21 +82,21 @@
 def pack(tiles, value):
     group = lane_index() // 8
     for r, tile in tiles:
-        turned = pltpu.roll(tile, (8 * r + 4) % LANES, 1)
-        value = jnp.where(group == r, turned, value)
+        value = jnp.where(group == r, pltpu.roll(tile, 8 * r + 4, 1), value)
     return value
 
 
-def prepare_kernel(mixing, low, high, held, own, old_sums, splat):
+def prepare_kernel(mixing, cross, chip, held, own, old_sums, splat):
     fields = held.shape[1]
     for f in range(fields):
         for g in range(fields):
             splat[f * fields + g] = jnp.full((8, LANES), mixing[f, g], jnp.float32)
     blank = jnp.zeros((8, LANES), jnp.float32)
+    side = STEPS * parity()
 
     def field(f, carry):
-        rows = [(STEPS + r, low[f, r]) for r in range(STEPS)]
-        rows += [(2 * STEPS + r, high[f, r]) for r in range(STEPS)]
+        rows = [(STEPS + side + r, cross[f, r]) for r in range(STEPS)]
+        rows += [(2 * STEPS - side + r, chip[f, r]) for r in range(STEPS)]
         own[f] = pack(rows, blank)
         return carry
 
@@ -98,14 +115,12 @@
         old_sums[i] = total
 
 
-def edges_kernel(before, after, own, packed):
-    def field(f, carry):
-        rows = [(r, before[f, r]) for r in range(STEPS)]
-        rows += [(3 * STEPS + r, after[f, r]) for r in range(STEPS)]
+def edges_kernel(from_cross, from_chip, own, packed):
+    side = 3 * STEPS * parity()
+    for f in range(own.shape[0]):
+        rows = [(side + r, from_cross[f, r]) for r in range(STEPS)]
+        rows += [(3 * STEPS - side + r, from_chip[f, r]) for r in range(STEPS)]
         packed[f] = pack(rows, own[f])
-        return carry
-
-    lax.fori_loop(0, own.shape[0], field, 0)
 
 
 def speeds(base, span):
@@ -140,28 +155,30 @@
             store(i, f, (near_x + near_z) + (near_y - 0.3 * v) + gain * mixed[i])
 
 
-def first_kernel(splat, before, low, high, after, made, coefs):
-    fields, rows = before.shape[0] - EXTRA, 4 * STEPS
-    parts = (before, low, high, after)
+def first_kernel(splat, from_cross, cross, chip, from_chip, made, coefs, slabs):
+    fields, rows = cross.shape[0] - EXTRA, 4 * STEPS
     lane, wall = lane_index(), walls()
-    for e in range(EXTRA):
-        for r in range(rows):
-            coefs[e, r] = parts[r // STEPS][fields + e, r % STEPS]
-
-    def tile(f, r):
-        return parts[r // STEPS][f, r % STEPS]
+    side = STEPS * parity()
+    for ref, row in (
+        (from_cross, 3 * side),
+        (cross, STEPS + side),
+        (chip, 2 * STEPS - side),
+        (from_chip, 3 * (STEPS - side)),
+    ):
+        slabs[:, pl.ds(row, STEPS)] = ref[...]
+    coefs[...] = slabs[fields:]
 
     def item(r):
-        values = [tile(f, r) for f in range(fields)]
+        values = [slabs[f, r] for f in range(fields)]
         return (
             values,
-            lambda f: tile(f, r + 1),
-            lambda f: tile(f, r - 1),
+            lambda f: slabs[f, r + 1],
+            lambda f: slabs[f, r - 1],
             lambda f: jnp.where(lane == LANES - 1, 0.0, pltpu.roll(values[f], LANES - 1, 1)),
             lambda f: jnp.where(lane == 0, 0.0, pltpu.roll(values[f], 1, 1)),
-            tile(fields, r),
-            tile(fields + 1, r),
-            tile(fields + 2, r),
+            slabs[fields, r],
+            slabs[fields + 1, r],
+            slabs[fields + 2, r],
         )
 
     for r in range(1, rows - 1, 2):
@@ -173,23 +190,23 @@
 
 
 def krylov_kernel(
-    splat, own, left, right, made, coefs, held, old_sums, krylov, sums, state, rim, inject
+    splat, own, left, right, made, coefs, held, old_sums, krylov, sums, outer_rows, rim, inject
 ):
     fields, rows = held.shape[1], 4 * STEPS
     lane, wall = lane_index(), walls()
     inner = lane % 8 < 4
 
-    def load(f, carry):
+    def place(k, r):
+        if STEPS <= r < 3 * STEPS:
+            return krylov.at[k], r - STEPS
+        return outer_rows.at[k % 2], r if r < STEPS else r - 2 * STEPS
+
+    for f in range(fields + EXTRA):
         mine = own[f]
         rim[0, f, 0] = jnp.where(inner, left[f], mine)
         rim[0, f, 1] = jnp.where(inner, mine, right[f])
-        return carry
-
-    lax.fori_loop(0, fields + EXTRA, load, 0)
 
     for k in range(STEPS):
-        src = state.at[k % 2]
-        dst = state.at[(k + 1) % 2]
         rim_src, rim_dst = rim.at[k % 2], rim.at[(k + 1) % 2]
         for f in range(fields):
             inject[f] = jnp.where(lane % 8 == 5, pltpu.roll(rim_src[f, 0], 2, 1), rim_src[f, 1])
@@ -217,24 +234,24 @@
             return pltpu.roll(inject[f], 123 - 8 * r, 1)
 
         if k == 0:
-
-            def fix(r, carry):
+            for r in range(1, rows - 1):
                 _, _, c_zu, c_zd = speeds(coefs[0, r], coefs[1, r])
                 scale = jnp.where(lane == LANES - 1, c_zu, jnp.where(lane == 0, c_zd, 0.0))
+                ref, at = place(0, r)
                 for f in range(fields):
-                    dst[f, r] = made[f, r] + scale * turned(f, r)
-                return carry
-
-            lax.fori_loop(1, rows - 1, fix, 0)
-            krylov[0] = dst[:, STEPS : 3 * STEPS]
+                    ref[f, at] = made[f, r] + scale * turned(f, r)
             continue
 
+        def tile(f, r):
+            ref, at = place(k - 1, r)
+            return ref[f, at]
+
         def item(r):
-            values = [src[f, r] for f in range(fields)]
+            values = [tile(f, r) for f in range(fields)]
             return (
                 values,
-                lambda f: src[f, r + 1],
-                lambda f: src[f, r - 1],
+                lambda f: tile(f, r + 1),
+                lambda f: tile(f, r - 1),
                 lambda f: jnp.where(
                     lane == LANES - 1, turned(f, r), pltpu.roll(values[f], LANES - 1, 1)
                 ),
@@ -244,17 +261,13 @@
                 coefs[2, r],
             )
 
-        def row(q, carry):
-            r = k + 1 + 2 * q
+        for r in range(k + 1, rows - k - 1, 2):
 
             def store(i, f, value):
-                dst[f, r + i] = value
+                ref, at = place(k, r + i)
+                ref[f, at] = value
 
             stencil(splat, [item(r), item(r + 1)], wall, store)
-            return carry
-
-        lax.fori_loop(0, (rows - 2 * k - 2) // 2, row, 0)
-        krylov[k] = dst[:, STEPS : 3 * STEPS]
 
     def products(f, totals):
         totals = list(totals)
@@ -349,19 +362,29 @@
                     value = value - lower[k, c] * made[c]
                 made.append(value * inverse[k])
                 buffer[k, f, x] = made[k]
-        out_copy(f).start()
         return carry
 
-    def out_copy(f):
-        return pltpu.make_async_copy(buffer.at[:, f], new_out.at[:, f], sems.at[f])
-
-    lax.fori_loop(0, fields, field, 0)
-    for f in range(fields):
-        out_copy(f).wait()
+    half = fields // 2
+    copies = []
+    for w in range(2):
+        lax.fori_loop(w * half, (w + 1) * half, field, 0)
+        span = pl.ds(w * half, half)
+        for k in range(STEPS):
+            copies.append(
+                pltpu.make_async_copy(buffer.at[k, span], new_out.at[k, span], sems.at[w, k])
+            )
+            copies[-1].start()
+    for copy in copies:
+        copy.wait()
 
 
 def far(*arrays):
     return [pltpu.with_memory_space_constraint(a, pltpu.HBM) for a in arrays]
+
+
+def swaps(size, first):
+    pairs = [(i, (i + 1) % size) for i in range(first, size, 2)]
+    return pairs + [(j, i) for i, j in pairs]
 
 
 def ring(axes, size):
@@ -390,7 +413,7 @@
     slab = kept(everything, STEPS, ny, nz)
     vectors = (count, fields, nx, ny, nz)
     params = pltpu.CompilerParams(vmem_limit_bytes=16 * 2**20)
-    low, high, held = pl.pallas_call(
+    cross, chip, held = pl.pallas_call(
         start_kernel,
         out_shape=(slab, slab, kept(*vectors)),
         in_specs=[HBM] * 5,
@@ -398,14 +421,15 @@
         scratch_shapes=[
             pltpu.SMEM((count,), jnp.float32),
             pltpu.SemaphoreType.DMA(()),
-            pltpu.SemaphoreType.DMA((fields,)),
+            pltpu.SemaphoreType.DMA((2, count)),
             pltpu.SemaphoreType.DMA((EXTRA, 2)),
         ],
         compiler_params=params,
         name="start",
     )(*far(coeffs, basis, base_speed, span_speed, polymer_gain))
-    up, down = ring(("outer", "inner"), outer * inner)
-    before, after = up(high), down(low)
+    stream = ("outer", "inner")
+    from_cross = lax.ppermute(cross, stream, swaps(outer * inner, 1))
+    from_chip = lax.ppermute(chip, stream, swaps(outer * inner, 0))
     own, old_sums, splat = pl.pallas_call(
         prepare_kernel,
         out_shape=(
@@ -417,7 +441,7 @@
         out_specs=(VMEM,) * 3,
         compiler_params=params,
         name="prepare",
-    )(mixing_matrix, *near(low, high, held))
+    )(mixing_matrix, *near(cross, chip, held))
     packed = pl.pallas_call(
         edges_kernel,
         out_shape=kept(everything, ny, nz),
@@ -425,7 +449,7 @@
         out_specs=VMEM,
         compiler_params=params,
         name="edges",
-    )(*near(before, after, own))
+    )(*near(from_cross, from_chip, own))
     up, down = ring("span", span)
     left, right = up(packed), down(packed)
     made, coefs = pl.pallas_call(
@@ -433,16 +457,17 @@
         out_shape=(kept(fields, 4 * STEPS, ny, nz), kept(EXTRA, 4 * STEPS, ny, nz)),
         in_specs=[VMEM] * 5,
         out_specs=(VMEM,) * 2,
+        scratch_shapes=[pltpu.VMEM((everything, 4 * STEPS, ny, nz), jnp.float32)],
         compiler_params=params,
         name="first",
-    )(*near(splat, before, low, high, after))
+    )(*near(splat, from_cross, cross, chip, from_chip))
     krylov, sums = pl.pallas_call(
         krylov_kernel,
         out_shape=(kept(*vectors), kept(inner, 1, nz)),
         in_specs=[VMEM] * 8,
         out_specs=(VMEM,) * 2,
         scratch_shapes=[
-            pltpu.VMEM((2, fields, 4 * STEPS, ny, nz), jnp.float32),
+            pltpu.VMEM((2, fields, 2 * STEPS, ny, nz), jnp.float32),
             pltpu.VMEM((2, everything, 2, ny, nz), jnp.float32),
             pltpu.VMEM((fields, ny, nz), jnp.float32),
         ],
@@ -459,7 +484,7 @@
         out_specs=(VMEM, VMEM, HBM),
         scratch_shapes=[
             pltpu.VMEM(vectors, jnp.float32),
-            pltpu.SemaphoreType.DMA((fields,)),
+            pltpu.SemaphoreType.DMA((2, STEPS)),
         ],
         compiler_params=params,
         name="finish",

time: 82.1 us -> 76 us (0.926)
  starting transfers between devices: 24.3 us -> 30.3 us
  waiting for transfers between devices: 8.34 us -> 3.23 us
  blocking collectives: 36.1 us -> 31.4 us
  Pallas kernels: 12.2 us -> 9.95 us
    ppermute x0 -> x2, starting transfers between devices: none -> 24 us  [the longest x1 18.6 us: on_device(): from_chip = lax.ppermute(chip, stream, swaps(outer * inner, 0))]
    ppermute x2 -> x1, starting transfers between devices: 20.4 us -> 4.39 us  [ring(): lax.ppermute(v, axes, down)]
    all_to_all x1, blocking collectives: 23.6 us -> 15.9 us  [on_device(): sums = lax.all_to_all(sums, 'inner', 0, 0, tiled=True)]
    ppermute x2 -> x1, waiting for transfers between devices: 8.34 us -> 3.23 us  [ring(): lax.ppermute(v, axes, up)]
    all_to_all x1, blocking collectives: 12.6 us -> 15.4 us  [on_device(): sums = lax.all_to_all(sums, ('outer', 'span'), 0, 0, tiled=True)]
    ppermute x2 -> x1, starting transfers between devices: 3.84 us -> 1.92 us  [ring(): lax.ppermute(v, axes, up)]
    pallas_call x1, Pallas kernels: 4.8 us -> 2.95 us  [on_device(): pl.pallas_call(krylov_kernel, out_shape=(kept(*vectors), kept(inner, 1, n...]
  transfers between devices with their start and end apart: 4 -> 4, of which waited for: 2 -> 1; matrix products, arithmetic and copies ran while one was open for 0% -> 0% of each run, Pallas kernels for 3% -> 4%
where the time goes in v3:
time: 76 us; the launch traced here: 75.7 us
  blocking collectives  31.4 us (41%)
  starting transfers between devices  30.3 us (40%)
  Pallas kernels  9.95 us (13%)
  waiting for transfers between devices  3.23 us (4%)
    ppermute x1, starting transfers between devices, on_device(): from_chip = lax.ppermute(chip, stream, swaps(outer * inner, 0))  18.6 us
    all_to_all x1, blocking collectives, on_device(): sums = lax.all_to_all(sums, 'inner', 0, 0, tiled=True)  15.9 us
    all_to_all x1, blocking collectives, on_device(): sums = lax.all_to_all(sums, ('outer', 'span'), 0, 0, tiled=True)  15.4 us
    ppermute x1, starting transfers between devices, on_device(): from_cross = lax.ppermute(cross, stream, swaps(outer * inner, 1))  5.39 us
    ppermute x1, starting transfers between devices, ring(): lax.ppermute(v, axes, down)  4.39 us
    ppermute x1, waiting for transfers between devices, ring(): lax.ppermute(v, axes, up)  3.23 us
    pallas_call x1, Pallas kernels, on_device(): pl.pallas_call(krylov_kernel, out_shape=(kept(*vectors), kept(inner, 1, n...  2.95 us
    pallas_call x1, Pallas kernels, on_device(): pl.pallas_call(functools.partial(finish_kernel, total), out_shape=(shape_...  2.26 us
  transfers between devices with their start and end apart: 4, of which 1 were waited for; matrix products, arithmetic and copies ran while one was open for 0% of the time, Pallas kernels for 4%

profile of v3, /device:TPU:1, one launch (start us, length us, event | category | flops | bytes accessed | tf_op | source)
XLA Modules:
  0.0 75.7 jit_solution(12103998719775798700)
XLA Ops:
  0.6 0.0 copy-start
  0.6 1.7 %start.1 = (f32[13,4,8,128]{3,2,1,0:T(8,128)S(1)}, f32[13,4,8,128]{3,2,1,0:T(8,128)S(1)}, f32[4,10,8,8,128]{4,3,2,1,0:T(8,128)S(1)}) custom-call(f32[4]{0:T(128)} %coeffs.1, f32[4,10,8,8,128]{4,3,2,1,0:T(8,128)} %basis.1, f32[8,8,128]{2,1,0:T(8,128)} %base_speed.1, f32[8,8,128]{2,1,0:T(8,128)} %span_speed.1, f32[8,8,128]{2,1,0:T(8,128)} %gain.1), custom_call_target="tpu_custom_call" | custom-call | tf_op jit(solution)/shard_map/start/pallas_call | solution.py:416
  2.3 5.4 %collective-permute-start = (f32[13,4,8,128]{3,2,1,0:T(8,128)S(1)}, f32[13,4,8,128]{3,2,1,0:T(8,128)S(1)}, u32[]{:S(2)}, u32[]{:S(2)}) collective-permute-start(f32[13,4,8,128]{3,2,1,0:T(8,128)S(1)} %get-tuple-element.13.cross), channel_id=1, source_target_pairs={{4,8},{12,16},{20,24},{28,32},{36,40},{44,48},{52,56},{60,64},{68,... | collective-permute-start | bytes 638984 | tf_op jit(solution)/shard_map/ppermute | solution.py:431
  7.7 18.6 %collective-permute-start.1 = (f32[13,4,8,128]{3,2,1,0:T(8,128)S(1)}, f32[13,4,8,128]{3,2,1,0:T(8,128)S(1)}, u32[]{:S(2)}, u32[]{:S(2)}) collective-permute-start(f32[13,4,8,128]{3,2,1,0:T(8,128)S(1)} %get-tuple-element.14.chip), channel_id=1, source_target_pairs={{0,4},{8,12},{16,20},{24,28},{32,36},{40,44},{48,52},{56,60},{64,6... | collective-permute-start | bytes 638984 | tf_op jit(solution)/shard_map/ppermute | solution.py:432
  26.3 0.0 copy-done
  26.3 2.0 %prepare.1 = (f32[13,8,128]{2,1,0:T(8,128)S(1)}, f32[10,8,128]{2,1,0:T(8,128)S(1)}, f32[100,8,128]{2,1,0:T(8,128)S(1)}) custom-call(f32[10,10]{1,0:T(8,128)S(1)} %copy-done, f32[13,4,8,128]{3,2,1,0:T(8,128)S(1)} %get-tuple-element.13.cross, f32[13,4,8,128]{3,2,1,0:T(8,128)S(1)} %get-tuple-element.14.chip, f32[4,10,8,8,128]{4,3,2,1,0:T(8,128)S(1)} %get-tuple-element.15.held.basis), custom_call_target="tpu_custom_call" | custom-call | tf_op jit(solution)/shard_map/prepare/pallas_call | solution.py:433
  28.3 0.0 collective-permute-done.from_cross
  28.3 0.0 collective-permute-done.1.from_chip
  28.3 0.2 edges.1.own
  28.5 4.4 %collective-permute-start.3 = (f32[13,8,128]{2,1,0:T(8,128)S(1)}, f32[13,8,128]{2,1,0:T(8,128)S(1)}, u32[]{:S(2)}, u32[]{:S(2)}) collective-permute-start(f32[13,8,128]{2,1,0:T(8,128)S(1)} %edges.1.own), channel_id=1, source_target_pairs={{1,0},{2,1},{3,2},{0,3},{5,4},{6,5},{7,6},{4,7},{9,8},{10,9},{11,1... | collective-permute-start | bytes 159752 | tf_op jit(solution)/shard_map/ppermute | solution.py:393
  32.9 1.9 %collective-permute-start.2 = (f32[13,8,128]{2,1,0:T(8,128)S(1)}, f32[13,8,128]{2,1,0:T(8,128)S(1)}, u32[]{:S(2)}, u32[]{:S(2)}) collective-permute-start(f32[13,8,128]{2,1,0:T(8,128)S(1)} %edges.1.own), channel_id=1, source_target_pairs={{0,1},{1,2},{2,3},{3,0},{4,5},{5,6},{6,7},{7,4},{8,9},{9,10},{10,1... | collective-permute-start | bytes 159752 | tf_op jit(solution)/shard_map/ppermute | solution.py:393
  34.8 0.9 %first.1 = (f32[10,16,8,128]{3,2,1,0:T(8,128)S(1)}, f32[3,16,8,128]{3,2,1,0:T(8,128)S(1)}) custom-call(f32[100,8,128]{2,1,0:T(8,128)S(1)} %get-tuple-element.16.splat, f32[13,4,8,128]{3,2,1,0:T(8,128)S(1)} %collective-permute-done.from_cross, f32[13,4,8,128]{3,2,1,0:T(8,128)S(1)} %get-tuple-element.13.cross, f32[13,4,8,128]{3,2,1,0:T(8,128)S(1)} %get-tuple-element.14.chip, ...), custom_call_target="tpu_custom_call" | custom-call | tf_op jit(solution)/shard_map/first/pallas_call | solution.py:455
  35.8 0.0 collective-permute-done.3.right
  35.8 3.2 %collective-permute-done.2.left = f32[13,8,128]{2,1,0:T(8,128)S(1)} collective-permute-done((f32[13,8,128]{2,1,0:T(8,128)S(1)}, f32[13,8,128]{2,1,0:T(8,128)S(1)}, u32[]{:S(2)}, u32[]{:S(2)}) %collective-permute-start.2) | collective-permute-done | bytes 53280 | tf_op jit(solution)/shard_map/ppermute | solution.py:393
  39.0 3.0 %krylov.1 = (f32[4,10,8,8,128]{4,3,2,1,0:T(8,128)S(1)}, f32[32,1,128]{2,1,0:T(1,128)S(1)}) custom-call(f32[100,8,128]{2,1,0:T(8,128)S(1)} %get-tuple-element.16.splat, f32[13,8,128]{2,1,0:T(8,128)S(1)} %edges.1.own, f32[13,8,128]{2,1,0:T(8,128)S(1)} %collective-permute-done.2.left, f32[13,8,128]{2,1,0:T(8,128)S(1)} %collective-permute-done.3.right, ...), custom_call_target="tpu_custom_call" | custom-call | tf_op jit(solution)/shard_map/krylov/pallas_call | solution.py:464
  42.0 15.9 %all_to_all.10 = f32[32,1,128]{2,1,0:T(1,128)S(1)} all-to-all(f32[32,1,128]{2,1,0:T(1,128)S(1)} %get-tuple-element.21), channel_id=1, replica_groups=mesh['outer'=8,'inner'=32,'span'=4] {'inner'}, dimensions={0} | all-to-all | bytes 32768 | tf_op jit(solution)/shard_map/all_to_all | solution.py:477
  57.9 0.1 reduce_sum.9
  58.0 15.4 %all_to_all.11.parts = f32[32,1,128]{2,1,0:T(1,128)S(1)} all-to-all(f32[32,1,128]{2,1,0:T(1,128)S(1)} %broadcast_in_dim.2), channel_id=1, replica_groups=mesh['outer'=8,'inner'=32,'span'=4] {'outer','span'}, dimensions={0} | all-to-all | bytes 32768 | tf_op jit(solution)/shard_map/all_to_all | solution.py:479
  73.4 2.3 %finish.1 = (f32[4,4]{1,0:T(4,128)}, f32[4,4]{1,0:T(4,128)}, f32[4,10,8,8,128]{4,3,2,1,0:T(8,128)}) custom-call(f32[32,1,128]{2,1,0:T(1,128)S(1)} %all_to_all.11.parts, f32[4,10,8,8,128]{4,3,2,1,0:T(8,128)S(1)} %get-tuple-element.22.krylov, f32[4,10,8,8,128]{4,3,2,1,0:T(8,128)S(1)} %get-tuple-element.15.held.basis), custom_call_target="tpu_custom_call" | custom-call | tf_op jit(solution)/shard_map/finish/pallas_call | solution.py:480
  (1 shorter events, 0.0 us)
Async XLA Ops:
  0.6 25.7 %copy-start = (f32[10,10]{1,0:T(8,128)S(1)}, f32[10,10]{1,0:T(8,128)}, u32[]{:S(2)}) copy-start(f32[10,10]{1,0:T(8,128)} %mixing.1) | copy-start | bytes 1204
  2.3 26.0 %collective-permute-start = (f32[13,4,8,128]{3,2,1,0:T(8,128)S(1)}, f32[13,4,8,128]{3,2,1,0:T(8,128)S(1)}, u32[]{:S(2)}, u32[]{:S(2)}) collective-permute-start(f32[13,4,8,128]{3,2,1,0:T(8,128)S(1)} %get-tuple-element.13.cross), channel_id=1, source_target_pairs={{4,8},{12,16},{20,24},{28,32},{36,40},{44,48},{52,56},{60,64},{68,... | collective-permute-start | bytes 638984 | tf_op jit(solution)/shard_map/ppermute | solution.py:431
  7.7 20.6 %collective-permute-start.1 = (f32[13,4,8,128]{3,2,1,0:T(8,128)S(1)}, f32[13,4,8,128]{3,2,1,0:T(8,128)S(1)}, u32[]{:S(2)}, u32[]{:S(2)}) collective-permute-start(f32[13,4,8,128]{3,2,1,0:T(8,128)S(1)} %get-tuple-element.14.chip), channel_id=1, source_target_pairs={{0,4},{8,12},{16,20},{24,28},{32,36},{40,44},{48,52},{56,60},{64,6... | collective-permute-start | bytes 638984 | tf_op jit(solution)/shard_map/ppermute | solution.py:432
  28.5 7.2 %collective-permute-start.3 = (f32[13,8,128]{2,1,0:T(8,128)S(1)}, f32[13,8,128]{2,1,0:T(8,128)S(1)}, u32[]{:S(2)}, u32[]{:S(2)}) collective-permute-start(f32[13,8,128]{2,1,0:T(8,128)S(1)} %edges.1.own), channel_id=1, source_target_pairs={{1,0},{2,1},{3,2},{0,3},{5,4},{6,5},{7,6},{4,7},{9,8},{10,9},{11,1... | collective-permute-start | bytes 159752 | tf_op jit(solution)/shard_map/ppermute | solution.py:393
  32.9 6.1 %collective-permute-start.2 = (f32[13,8,128]{2,1,0:T(8,128)S(1)}, f32[13,8,128]{2,1,0:T(8,128)S(1)}, u32[]{:S(2)}, u32[]{:S(2)}) collective-permute-start(f32[13,8,128]{2,1,0:T(8,128)S(1)} %edges.1.own), channel_id=1, source_target_pairs={{0,1},{1,2},{2,3},{3,0},{4,5},{5,6},{6,7},{7,4},{8,9},{9,10},{10,1... | collective-permute-start | bytes 159752 | tf_op jit(solution)/shard_map/ppermute | solution.py:393

commit v4 on v3

--- a/solution.py
+++ b/solution.py
@@ -86,41 +86,27 @@
     return value
 
 
-def prepare_kernel(mixing, cross, chip, held, own, old_sums, splat):
-    fields = held.shape[1]
-    for f in range(fields):
-        for g in range(fields):
-            splat[f * fields + g] = jnp.full((8, LANES), mixing[f, g], jnp.float32)
-    blank = jnp.zeros((8, LANES), jnp.float32)
+def own_edges_kernel(cross, chip, own):
     side = STEPS * parity()
-
-    def field(f, carry):
+    for f in range(own.shape[0]):
         rows = [(STEPS + side + r, cross[f, r]) for r in range(STEPS)]
         rows += [(2 * STEPS - side + r, chip[f, r]) for r in range(STEPS)]
-        own[f] = pack(rows, blank)
-        return carry
-
-    lax.fori_loop(0, own.shape[0], field, 0)
-
-    def products(f, totals):
-        totals = list(totals)
-        for x in range(2 * STEPS):
-            old = [held[m, f, x] for m in range(STEPS)]
-            for i, (a, b) in enumerate(PAIRS):
-                totals[i] = totals[i] + old[a] * old[b]
-        return tuple(totals)
-
-    totals = lax.fori_loop(0, fields, products, (blank,) * len(PAIRS))
-    for i, total in enumerate(totals):
-        old_sums[i] = total
-
-
-def edges_kernel(from_cross, from_chip, own, packed):
+        own[f] = pack(rows, jnp.zeros((8, LANES), jnp.float32))
+
+
+def edges_kernel(from_cross, from_chip, own, packed, to_right, to_left):
     side = 3 * STEPS * parity()
+    made = []
     for f in range(own.shape[0]):
         rows = [(side + r, from_cross[f, r]) for r in range(STEPS)]
         rows += [(3 * STEPS - side + r, from_chip[f, r]) for r in range(STEPS)]
-        packed[f] = pack(rows, own[f])
+        made.append(pack(rows, own[f]))
+        packed[f] = made[f]
+    inner = lane_index() % 8 < 4
+    for q in range(to_right.shape[0]):
+        even, odd = made[2 * q], made[min(2 * q + 1, len(made) - 1)]
+        to_right[q] = jnp.where(inner, even, pltpu.roll(odd, 4, 1))
+        to_left[q] = jnp.where(inner, pltpu.roll(odd, LANES - 4, 1), even)
 
 
 def speeds(base, span):
@@ -155,10 +141,15 @@
             store(i, f, (near_x + near_z) + (near_y - 0.3 * v) + gain * mixed[i])
 
 
-def first_kernel(splat, from_cross, cross, chip, from_chip, made, coefs, slabs):
+def first_kernel(
+    mixing, from_cross, cross, chip, from_chip, held, made, coefs, splat, old_sums, slabs
+):
     fields, rows = cross.shape[0] - EXTRA, 4 * STEPS
     lane, wall = lane_index(), walls()
     side = STEPS * parity()
+    for f in range(fields):
+        for g in range(fields):
+            splat[f * fields + g] = jnp.full((8, LANES), mixing[f, g], jnp.float32)
     for ref, row in (
         (from_cross, 3 * side),
         (cross, STEPS + side),
@@ -188,9 +179,21 @@
 
         stencil(splat, [item(r), item(r + 1)], wall, store)
 
+    def products(f, totals):
+        totals = list(totals)
+        for x in range(2 * STEPS):
+            old = [held[m, f, x] for m in range(STEPS)]
+            for i, (a, b) in enumerate(PAIRS):
+                totals[i] = totals[i] + old[a] * old[b]
+        return tuple(totals)
+
+    blank = jnp.zeros((8, LANES), jnp.float32)
+    for i, total in enumerate(lax.fori_loop(0, fields, products, (blank,) * len(PAIRS))):
+        old_sums[i] = total
+
 
 def krylov_kernel(
-    splat, own, left, right, made, coefs, held, old_sums, krylov, sums, outer_rows, rim, inject
+    splat, own, from_left, from_right, made, coefs, held, old_sums, krylov, sums, outer_rows, rim, inject
 ):
     fields, rows = held.shape[1], 4 * STEPS
     lane, wall = lane_index(), walls()
@@ -202,9 +205,11 @@
         return outer_rows.at[k % 2], r if r < STEPS else r - 2 * STEPS
 
     for f in range(fields + EXTRA):
-        mine = own[f]
-        rim[0, f, 0] = jnp.where(inner, left[f], mine)
-        rim[0, f, 1] = jnp.where(inner, mine, right[f])
+        mine, left, right = own[f], from_left[f // 2], from_right[f // 2]
+        if f % 2:
+            left, right = pltpu.roll(left, LANES - 4, 1), pltpu.roll(right, 4, 1)
+        rim[0, f, 0] = jnp.where(inner, left, mine)
+        rim[0, f, 1] = jnp.where(inner, mine, right)
 
     for k in range(STEPS):
         rim_src, rim_dst = rim.at[k % 2], rim.at[(k + 1) % 2]
@@ -285,7 +290,9 @@
         return tuple(totals)
 
     zero = jnp.zeros((8, LANES), jnp.float32)
-    totals = lax.fori_loop(0, fields, products, (zero,) * (STEPS * STEPS + len(PAIRS)))
+    totals = (zero,) * (STEPS * STEPS + len(PAIRS))
+    for f in range(fields):
+        totals = products(f, totals)
     totals = list(totals) + [old_sums[i] for i in range(len(PAIRS))]
     lines = [jnp.sum(t, axis=0, keepdims=True) for t in totals]
     lines.append(jnp.zeros((LANES - len(lines), LANES), jnp.float32))
@@ -301,7 +308,7 @@
         sums[i] = row_sums[0:1]
 
 
-def finish_kernel(total, parts, krylov, basis, proj_out, factor_out, new_out, buffer, sems):
+def finish_kernel(total, parts, krylov, basis, proj_out, factor_out, new_out):
     fields = basis.shape[1]
     line = parts[0]
     for i in range(1, parts.shape[0]):
@@ -334,8 +341,8 @@
             for c in range(b):
                 value = value - lower[a, c] * lower[b, c]
             if a == b:
-                lower[a, b] = jnp.sqrt(value)
-                inverse.append(1.0 / lower[a, b])
+                inverse.append(lax.rsqrt(value))
+                lower[a, b] = value * inverse[b]
             else:
                 lower[a, b] = value * inverse[b]
     lane, sub = lane_index(), row_index()
@@ -361,21 +368,10 @@
                 for c in range(k):
                     value = value - lower[k, c] * made[c]
                 made.append(value * inverse[k])
-                buffer[k, f, x] = made[k]
+                new_out[k, f, x] = made[k]
         return carry
 
-    half = fields // 2
-    copies = []
-    for w in range(2):
-        lax.fori_loop(w * half, (w + 1) * half, field, 0)
-        span = pl.ds(w * half, half)
-        for k in range(STEPS):
-            copies.append(
-                pltpu.make_async_copy(buffer.at[k, span], new_out.at[k, span], sems.at[w, k])
-            )
-            copies[-1].start()
-    for copy in copies:
-        copy.wait()
+    lax.fori_loop(0, fields, field, 0)
 
 
 def far(*arrays):
@@ -430,37 +426,39 @@
     stream = ("outer", "inner")
     from_cross = lax.ppermute(cross, stream, swaps(outer * inner, 1))
     from_chip = lax.ppermute(chip, stream, swaps(outer * inner, 0))
-    own, old_sums, splat = pl.pallas_call(
-        prepare_kernel,
-        out_shape=(
-            kept(everything, ny, nz),
-            kept(len(PAIRS), ny, nz),
-            kept(fields * fields, ny, nz),
-        ),
-        in_specs=[SMEM] + [VMEM] * 3,
+    own = pl.pallas_call(
+        own_edges_kernel,
+        out_shape=kept(everything, ny, nz),
+        in_specs=[VMEM] * 2,
+        out_specs=VMEM,
+        compiler_params=params,
+        name="own_edges",
+    )(*near(cross, chip))
+    halves = kept((everything + 1) // 2, ny, nz)
+    packed, to_right, to_left = pl.pallas_call(
+        edges_kernel,
+        out_shape=(kept(everything, ny, nz), halves, halves),
+        in_specs=[VMEM] * 3,
         out_specs=(VMEM,) * 3,
-        compiler_params=params,
-        name="prepare",
-    )(mixing_matrix, *near(cross, chip, held))
-    packed = pl.pallas_call(
-        edges_kernel,
-        out_shape=kept(everything, ny, nz),
-        in_specs=[VMEM] * 3,
-        out_specs=VMEM,
         compiler_params=params,
         name="edges",
     )(*near(from_cross, from_chip, own))
     up, down = ring("span", span)
-    left, right = up(packed), down(packed)
-    made, coefs = pl.pallas_call(
+    from_left, from_right = up(to_right), down(to_left)
+    made, coefs, splat, old_sums = pl.pallas_call(
         first_kernel,
-        out_shape=(kept(fields, 4 * STEPS, ny, nz), kept(EXTRA, 4 * STEPS, ny, nz)),
-        in_specs=[VMEM] * 5,
-        out_specs=(VMEM,) * 2,
+        out_shape=(
+            kept(fields, 4 * STEPS, ny, nz),
+            kept(EXTRA, 4 * STEPS, ny, nz),
+            kept(fields * fields, ny, nz),
+            kept(len(PAIRS), ny, nz),
+        ),
+        in_specs=[SMEM] + [VMEM] * 5,
+        out_specs=(VMEM,) * 4,
         scratch_shapes=[pltpu.VMEM((everything, 4 * STEPS, ny, nz), jnp.float32)],
         compiler_params=params,
         name="first",
-    )(*near(splat, from_cross, cross, chip, from_chip))
+    )(mixing_matrix, *near(from_cross, cross, chip, from_chip, held))
     krylov, sums = pl.pallas_call(
         krylov_kernel,
         out_shape=(kept(*vectors), kept(inner, 1, nz)),
@@ -473,7 +471,7 @@
         ],
         compiler_params=params,
         name="krylov",
-    )(*near(splat, packed, left, right, made, coefs, held, old_sums))
+    )(*near(splat, packed, from_left, from_right, made, coefs, held, old_sums))
     sums = lax.all_to_all(sums, "inner", 0, 0, tiled=True)
     sums = jnp.broadcast_to(jnp.sum(sums, axis=0, keepdims=True), (outer * span, 1, nz))
     sums = lax.all_to_all(sums, ("outer", "span"), 0, 0, tiled=True)
@@ -481,11 +479,7 @@
         functools.partial(finish_kernel, total),
         out_shape=(shape_of(count, STEPS), shape_of(STEPS, STEPS), shape_of(*vectors)),
         in_specs=[VMEM] * 3,
-        out_specs=(VMEM, VMEM, HBM),
-        scratch_shapes=[
-            pltpu.VMEM(vectors, jnp.float32),
-            pltpu.SemaphoreType.DMA((2, STEPS)),
-        ],
+        out_specs=(VMEM,) * 3,
         compiler_params=params,
         name="finish",
     )(*near(sums, krylov, held))

time: 76 us -> 75.1 us (0.988)
  blocking collectives: 31.4 us -> 34.1 us
  waiting for transfers between devices: 3.23 us -> 0.88 us
  Pallas kernels: 9.95 us -> 8.53 us
    ppermute x1, waiting for transfers between devices: 3.23 us -> 0.01 us  [ring(): lax.ppermute(v, axes, up)]
    all_to_all x1, blocking collectives: 15.4 us -> 18 us  [on_device(): sums = lax.all_to_all(sums, ('outer', 'span'), 0, 0, tiled=True)]
    pallas_call x2, Pallas kernels: 2.15 us -> 0.42 us  [the longest x1 0.23 us: on_device(): pl.pallas_call(edges_kernel, out_shape=(kept(everything, ny, nz), halves,...]
    ppermute x1, starting transfers between devices: 1.92 us -> 3.11 us  [ring(): lax.ppermute(v, axes, up)]
    ppermute x1, starting transfers between devices: 4.39 us -> 3.37 us  [ring(): lax.ppermute(v, axes, down)]
    ppermute x1, waiting for transfers between devices: 0.01 us -> 0.87 us  [on_device(): from_chip = lax.ppermute(chip, stream, swaps(outer * inner, 0))]
    pallas_call x1, Pallas kernels: 0.92 us -> 1.78 us  [on_device(): pl.pallas_call(first_kernel, out_shape=(kept(fields, 4 * STEPS, ny, nz),...]
  transfers between devices with their start and end apart: 4 -> 4, of which waited for: 1 -> 1; matrix products, arithmetic and copies ran while one was open for 0% -> 0% of each run, Pallas kernels for 4% -> 3%
where the time goes in v4:
time: 75.1 us; the launch traced here: 74.8 us
  blocking collectives  34.1 us (45%)
  starting transfers between devices  30.5 us (41%)
  Pallas kernels  8.53 us (11%)
  waiting for transfers between devices  0.88 us (1%)
    ppermute x1, starting transfers between devices, on_device(): from_chip = lax.ppermute(chip, stream, swaps(outer * inner, 0))  18.6 us
    all_to_all x1, blocking collectives, on_device(): sums = lax.all_to_all(sums, ('outer', 'span'), 0, 0, tiled=True)  18 us
    all_to_all x1, blocking collectives, on_device(): sums = lax.all_to_all(sums, 'inner', 0, 0, tiled=True)  16.1 us
    ppermute x1, starting transfers between devices, on_device(): from_cross = lax.ppermute(cross, stream, swaps(outer * inner, 1))  5.39 us
    ppermute x1, starting transfers between devices, ring(): lax.ppermute(v, axes, down)  3.37 us
    ppermute x1, starting transfers between devices, ring(): lax.ppermute(v, axes, up)  3.11 us
    pallas_call x1, Pallas kernels, on_device(): pl.pallas_call(krylov_kernel, out_shape=(kept(*vectors), kept(inner, 1, n...  2.85 us
    pallas_call x1, Pallas kernels, on_device(): pl.pallas_call(functools.partial(finish_kernel, total), out_shape=(shape_...  1.82 us
  transfers between devices with their start and end apart: 4, of which 1 were waited for; matrix products, arithmetic and copies ran while one was open for 0% of the time, Pallas kernels for 3%

profile of v4, /device:TPU:1, one launch (start us, length us, event | category | flops | bytes accessed | tf_op | source)
XLA Modules:
  0.0 74.8 jit_solution(12182412558205907227)
XLA Ops:
  0.6 0.0 copy-start
  0.6 1.7 %start.1 = (f32[13,4,8,128]{3,2,1,0:T(8,128)S(1)}, f32[13,4,8,128]{3,2,1,0:T(8,128)S(1)}, f32[4,10,8,8,128]{4,3,2,1,0:T(8,128)S(1)}) custom-call(f32[4]{0:T(128)} %coeffs.1, f32[4,10,8,8,128]{4,3,2,1,0:T(8,128)} %basis.1, f32[8,8,128]{2,1,0:T(8,128)} %base_speed.1, f32[8,8,128]{2,1,0:T(8,128)} %span_speed.1, f32[8,8,128]{2,1,0:T(8,128)} %gain.1), custom_call_target="tpu_custom_call" | custom-call | tf_op jit(solution)/shard_map/start/pallas_call | solution.py:412
  2.3 5.4 %collective-permute-start = (f32[13,4,8,128]{3,2,1,0:T(8,128)S(1)}, f32[13,4,8,128]{3,2,1,0:T(8,128)S(1)}, u32[]{:S(2)}, u32[]{:S(2)}) collective-permute-start(f32[13,4,8,128]{3,2,1,0:T(8,128)S(1)} %get-tuple-element.15.cross), channel_id=1, source_target_pairs={{4,8},{12,16},{20,24},{28,32},{36,40},{44,48},{52,56},{60,64},{68,... | collective-permute-start | bytes 638984 | tf_op jit(solution)/shard_map/ppermute | solution.py:427
  7.7 18.6 %collective-permute-start.1 = (f32[13,4,8,128]{3,2,1,0:T(8,128)S(1)}, f32[13,4,8,128]{3,2,1,0:T(8,128)S(1)}, u32[]{:S(2)}, u32[]{:S(2)}) collective-permute-start(f32[13,4,8,128]{3,2,1,0:T(8,128)S(1)} %get-tuple-element.16.chip), channel_id=1, source_target_pairs={{0,4},{8,12},{16,20},{24,28},{32,36},{40,44},{48,52},{56,60},{64,6... | collective-permute-start | bytes 638984 | tf_op jit(solution)/shard_map/ppermute | solution.py:428
  26.3 0.2 own_edges.1.own
  26.5 0.0 collective-permute-done.from_cross
  26.5 0.9 %collective-permute-done.1.from_chip = f32[13,4,8,128]{3,2,1,0:T(8,128)S(1)} collective-permute-done((f32[13,4,8,128]{3,2,1,0:T(8,128)S(1)}, f32[13,4,8,128]{3,2,1,0:T(8,128)S(1)}, u32[]{:S(2)}, u32[]{:S(2)}) %collective-permute-start.1) | collective-permute-done | bytes 213024 | tf_op jit(solution)/shard_map/ppermute | solution.py:428
  27.4 0.2 edges.1
  27.6 3.1 %collective-permute-start.2 = (f32[7,8,128]{2,1,0:T(8,128)S(1)}, f32[7,8,128]{2,1,0:T(8,128)S(1)}, u32[]{:S(2)}, u32[]{:S(2)}) collective-permute-start(f32[7,8,128]{2,1,0:T(8,128)S(1)} %get-tuple-element.20), channel_id=1, source_target_pairs={{0,1},{1,2},{2,3},{3,0},{4,5},{5,6},{6,7},{7,4},{8,9},{9,10},{10,1... | collective-permute-start | bytes 86024 | tf_op jit(solution)/shard_map/ppermute | solution.py:389
  30.7 3.4 %collective-permute-start.3 = (f32[7,8,128]{2,1,0:T(8,128)S(1)}, f32[7,8,128]{2,1,0:T(8,128)S(1)}, u32[]{:S(2)}, u32[]{:S(2)}) collective-permute-start(f32[7,8,128]{2,1,0:T(8,128)S(1)} %get-tuple-element.21), channel_id=1, source_target_pairs={{1,0},{2,1},{3,2},{0,3},{5,4},{6,5},{7,6},{4,7},{9,8},{10,9},{11,1... | collective-permute-start | bytes 86024 | tf_op jit(solution)/shard_map/ppermute | solution.py:389
  34.1 0.0 copy-done
  34.1 1.8 %first.1 = (f32[10,16,8,128]{3,2,1,0:T(8,128)S(1)}, f32[3,16,8,128]{3,2,1,0:T(8,128)S(1)}, f32[100,8,128]{2,1,0:T(8,128)S(1)}, f32[10,8,128]{2,1,0:T(8,128)S(1)}) custom-call(f32[10,10]{1,0:T(8,128)S(1)} %copy-done, f32[13,4,8,128]{3,2,1,0:T(8,128)S(1)} %collective-permute-done.from_cross, f32[13,4,8,128]{3,2,1,0:T(8,128)S(1)} %get-tuple-element.15.cross, ...), custom_call_target="tpu_custom_call" | custom-call | tf_op jit(solution)/shard_map/first/pallas_call | solution.py:448
  35.9 0.0 collective-permute-done.2.from_left
  35.9 0.0 collective-permute-done.3.from_right
  35.9 2.8 %krylov.1 = (f32[4,10,8,8,128]{4,3,2,1,0:T(8,128)S(1)}, f32[32,1,128]{2,1,0:T(1,128)S(1)}) custom-call(f32[100,8,128]{2,1,0:T(8,128)S(1)} %get-tuple-element.18.splat, f32[13,8,128]{2,1,0:T(8,128)S(1)} %get-tuple-element.19.own, f32[7,8,128]{2,1,0:T(8,128)S(1)} %collective-permute-done.2.from_left, f32[7,8,128]{2,1,0:T(8,128)S(1)} %collective-permute-done.3.from_right, ...), custom_call_target="tpu_custom_call" | custom-call | tf_op jit(solution)/shard_map/krylov/pallas_call | solution.py:462
  38.8 16.1 %all_to_all.10 = f32[32,1,128]{2,1,0:T(1,128)S(1)} all-to-all(f32[32,1,128]{2,1,0:T(1,128)S(1)} %get-tuple-element.25), channel_id=1, replica_groups=mesh['outer'=8,'inner'=32,'span'=4] {'inner'}, dimensions={0} | all-to-all | bytes 32768 | tf_op jit(solution)/shard_map/all_to_all | solution.py:475
  54.9 0.1 reduce_sum.9
  55.0 18.0 %all_to_all.11.parts = f32[32,1,128]{2,1,0:T(1,128)S(1)} all-to-all(f32[32,1,128]{2,1,0:T(1,128)S(1)} %broadcast_in_dim.2), channel_id=1, replica_groups=mesh['outer'=8,'inner'=32,'span'=4] {'outer','span'}, dimensions={0} | all-to-all | bytes 32768 | tf_op jit(solution)/shard_map/all_to_all | solution.py:477
  73.0 1.8 %finish.1 = (f32[4,4]{1,0:T(4,128)}, f32[4,4]{1,0:T(4,128)}, f32[4,10,8,8,128]{4,3,2,1,0:T(8,128)}) custom-call(f32[32,1,128]{2,1,0:T(1,128)S(1)} %all_to_all.11.parts, f32[4,10,8,8,128]{4,3,2,1,0:T(8,128)S(1)} %get-tuple-element.26.krylov, f32[4,10,8,8,128]{4,3,2,1,0:T(8,128)S(1)} %get-tuple-element.17.held.basis), custom_call_target="tpu_custom_call" | custom-call | tf_op jit(solution)/shard_map/finish/pallas_call | solution.py:478
  (1 shorter events, 0.0 us)
Async XLA Ops:
  0.6 33.5 %copy-start = (f32[10,10]{1,0:T(8,128)S(1)}, f32[10,10]{1,0:T(8,128)}, u32[]{:S(2)}) copy-start(f32[10,10]{1,0:T(8,128)} %mixing.1) | copy-start | bytes 1204
  2.3 24.2 %collective-permute-start = (f32[13,4,8,128]{3,2,1,0:T(8,128)S(1)}, f32[13,4,8,128]{3,2,1,0:T(8,128)S(1)}, u32[]{:S(2)}, u32[]{:S(2)}) collective-permute-start(f32[13,4,8,128]{3,2,1,0:T(8,128)S(1)} %get-tuple-element.15.cross), channel_id=1, source_target_pairs={{4,8},{12,16},{20,24},{28,32},{36,40},{44,48},{52,56},{60,64},{68,... | collective-permute-start | bytes 638984 | tf_op jit(solution)/shard_map/ppermute | solution.py:427
  7.7 19.7 %collective-permute-start.1 = (f32[13,4,8,128]{3,2,1,0:T(8,128)S(1)}, f32[13,4,8,128]{3,2,1,0:T(8,128)S(1)}, u32[]{:S(2)}, u32[]{:S(2)}) collective-permute-start(f32[13,4,8,128]{3,2,1,0:T(8,128)S(1)} %get-tuple-element.16.chip), channel_id=1, source_target_pairs={{0,4},{8,12},{16,20},{24,28},{32,36},{40,44},{48,52},{56,60},{64,6... | collective-permute-start | bytes 638984 | tf_op jit(solution)/shard_map/ppermute | solution.py:428
  27.6 8.3 %collective-permute-start.2 = (f32[7,8,128]{2,1,0:T(8,128)S(1)}, f32[7,8,128]{2,1,0:T(8,128)S(1)}, u32[]{:S(2)}, u32[]{:S(2)}) collective-permute-start(f32[7,8,128]{2,1,0:T(8,128)S(1)} %get-tuple-element.20), channel_id=1, source_target_pairs={{0,1},{1,2},{2,3},{3,0},{4,5},{5,6},{6,7},{7,4},{8,9},{9,10},{10,1... | collective-permute-start | bytes 86024 | tf_op jit(solution)/shard_map/ppermute | solution.py:389
  30.7 5.2 %collective-permute-start.3 = (f32[7,8,128]{2,1,0:T(8,128)S(1)}, f32[7,8,128]{2,1,0:T(8,128)S(1)}, u32[]{:S(2)}, u32[]{:S(2)}) collective-permute-start(f32[7,8,128]{2,1,0:T(8,128)S(1)} %get-tuple-element.21), channel_id=1, source_target_pairs={{1,0},{2,1},{3,2},{0,3},{5,4},{6,5},{7,6},{4,7},{9,8},{10,9},{11,1... | collective-permute-start | bytes 86024 | tf_op jit(solution)/shard_map/ppermute | solution.py:389

commit v5 on v4

--- a/solution.py
+++ b/solution.py
@@ -86,12 +86,27 @@
     return value
 
 
-def own_edges_kernel(cross, chip, own):
-    side = STEPS * parity()
+def prepare_kernel(mixing, cross, chip, held, own, splat, old_sums):
+    fields, side = held.shape[1], STEPS * parity()
+    blank = jnp.zeros((8, LANES), jnp.float32)
     for f in range(own.shape[0]):
         rows = [(STEPS + side + r, cross[f, r]) for r in range(STEPS)]
         rows += [(2 * STEPS - side + r, chip[f, r]) for r in range(STEPS)]
-        own[f] = pack(rows, jnp.zeros((8, LANES), jnp.float32))
+        own[f] = pack(rows, blank)
+    for f in range(fields):
+        for g in range(fields):
+            splat[f * fields + g] = jnp.full((8, LANES), mixing[f, g], jnp.float32)
+
+    def products(f, totals):
+        totals = list(totals)
+        for x in range(2 * STEPS):
+            old = [held[m, f, x] for m in range(STEPS)]
+            for i, (a, b) in enumerate(PAIRS):
+                totals[i] = totals[i] + old[a] * old[b]
+        return tuple(totals)
+
+    for i, total in enumerate(lax.fori_loop(0, fields, products, (blank,) * len(PAIRS))):
+        old_sums[i] = total
 
 
 def edges_kernel(from_cross, from_chip, own, packed, to_right, to_left):
@@ -141,15 +156,10 @@
             store(i, f, (near_x + near_z) + (near_y - 0.3 * v) + gain * mixed[i])
 
 
-def first_kernel(
-    mixing, from_cross, cross, chip, from_chip, held, made, coefs, splat, old_sums, slabs
-):
+def alone_kernel(splat, from_cross, cross, chip, from_chip, made, slabs, outer_rows):
     fields, rows = cross.shape[0] - EXTRA, 4 * STEPS
     lane, wall = lane_index(), walls()
     side = STEPS * parity()
-    for f in range(fields):
-        for g in range(fields):
-            splat[f * fields + g] = jnp.full((8, LANES), mixing[f, g], jnp.float32)
     for ref, row in (
         (from_cross, 3 * side),
         (cross, STEPS + side),
@@ -157,53 +167,49 @@
         (from_chip, 3 * (STEPS - side)),
     ):
         slabs[:, pl.ds(row, STEPS)] = ref[...]
-    coefs[...] = slabs[fields:]
-
-    def item(r):
-        values = [slabs[f, r] for f in range(fields)]
-        return (
-            values,
-            lambda f: slabs[f, r + 1],
-            lambda f: slabs[f, r - 1],
-            lambda f: jnp.where(lane == LANES - 1, 0.0, pltpu.roll(values[f], LANES - 1, 1)),
-            lambda f: jnp.where(lane == 0, 0.0, pltpu.roll(values[f], 1, 1)),
-            slabs[fields, r],
-            slabs[fields + 1, r],
-            slabs[fields + 2, r],
-        )
-
-    for r in range(1, rows - 1, 2):
-
-        def store(i, f, value, r=r):
-            made[f, r + i] = value
-
-        stencil(splat, [item(r), item(r + 1)], wall, store)
-
-    def products(f, totals):
-        totals = list(totals)
-        for x in range(2 * STEPS):
-            old = [held[m, f, x] for m in range(STEPS)]
-            for i, (a, b) in enumerate(PAIRS):
-                totals[i] = totals[i] + old[a] * old[b]
-        return tuple(totals)
-
-    blank = jnp.zeros((8, LANES), jnp.float32)
-    for i, total in enumerate(lax.fori_loop(0, fields, products, (blank,) * len(PAIRS))):
-        old_sums[i] = total
+
+    def place(k, r):
+        if k < 0:
+            return slabs, r
+        if STEPS <= r < 3 * STEPS:
+            return made.at[k], r - STEPS
+        return outer_rows.at[k % 2], r if r < STEPS else r - 2 * STEPS
+
+    for k in range(STEPS):
+
+        def tile(f, r):
+            ref, at = place(k - 1, r)
+            return ref[f, at]
+
+        def item(r):
+            values = [tile(f, r) for f in range(fields)]
+            return (
+                values,
+                lambda f: tile(f, r + 1),
+                lambda f: tile(f, r - 1),
+                lambda f: jnp.where(lane == LANES - 1, 0.0, pltpu.roll(values[f], LANES - 1, 1)),
+                lambda f: jnp.where(lane == 0, 0.0, pltpu.roll(values[f], 1, 1)),
+                slabs[fields, r],
+                slabs[fields + 1, r],
+                slabs[fields + 2, r],
+            )
+
+        for r in range(k + 1, rows - k - 1, 2):
+
+            def store(i, f, value):
+                ref, at = place(k, r + i)
+                ref[f, at] = value
+
+            stencil(splat, [item(r), item(r + 1)], wall, store)
 
 
 def krylov_kernel(
-    splat, own, from_left, from_right, made, coefs, held, old_sums, krylov, sums, outer_rows, rim, inject
+    splat, own, from_left, from_right, made, held, old_sums, krylov, sums, rim, change
 ):
-    fields, rows = held.shape[1], 4 * STEPS
+    fields = held.shape[1]
     lane, wall = lane_index(), walls()
-    inner = lane % 8 < 4
-
-    def place(k, r):
-        if STEPS <= r < 3 * STEPS:
-            return krylov.at[k], r - STEPS
-        return outer_rows.at[k % 2], r if r < STEPS else r - 2 * STEPS
-
+    place = lane % 8
+    inner = place < 4
     for f in range(fields + EXTRA):
         mine, left, right = own[f], from_left[f // 2], from_right[f // 2]
         if f % 2:
@@ -211,73 +217,62 @@
         rim[0, f, 0] = jnp.where(inner, left, mine)
         rim[0, f, 1] = jnp.where(inner, mine, right)
 
+    _, _, c_zu, c_zd = speeds(own[fields], own[fields + 1])
+    c_zu, c_zd = jnp.where(place == 3, c_zu, 0.0), jnp.where(place == 4, c_zd, 0.0)
+    for f in range(fields):
+        change[0, f] = c_zu * pltpu.roll(rim[0, f, 1], LANES - 1, 1) + c_zd * pltpu.roll(rim[0, f, 0], 1, 1)
+
     for k in range(STEPS):
-        rim_src, rim_dst = rim.at[k % 2], rim.at[(k + 1) % 2]
-        for f in range(fields):
-            inject[f] = jnp.where(lane % 8 == 5, pltpu.roll(rim_src[f, 0], 2, 1), rim_src[f, 1])
-        if k + 1 < STEPS:
-
-            def edge(e):
-                values = [rim_src[f, e] for f in range(fields)]
-                return (
-                    values,
-                    lambda f: pltpu.roll(values[f], LANES - 8, 1),
-                    lambda f: pltpu.roll(values[f], 8, 1),
-                    lambda f: pltpu.roll(values[f], LANES - 1, 1),
-                    lambda f: pltpu.roll(values[f], 1, 1),
-                    rim[0, fields, e],
-                    rim[0, fields + 1, e],
-                    rim[0, fields + 2, e],
-                )
-
-            def edge_store(i, f, value):
-                rim_dst[f, i] = value
-
-            stencil(splat, [edge(0), edge(1)], wall, edge_store)
-
-        def turned(f, r):
-            return pltpu.roll(inject[f], 123 - 8 * r, 1)
-
-        if k == 0:
-            for r in range(1, rows - 1):
-                _, _, c_zu, c_zd = speeds(coefs[0, r], coefs[1, r])
-                scale = jnp.where(lane == LANES - 1, c_zu, jnp.where(lane == 0, c_zd, 0.0))
-                ref, at = place(0, r)
-                for f in range(fields):
-                    ref[f, at] = made[f, r] + scale * turned(f, r)
-            continue
-
-        def tile(f, r):
-            ref, at = place(k - 1, r)
-            return ref[f, at]
-
-        def item(r):
-            values = [tile(f, r) for f in range(fields)]
+
+        def edge(e):
+            values = [rim[k, f, e] for f in range(fields)]
             return (
                 values,
-                lambda f: tile(f, r + 1),
-                lambda f: tile(f, r - 1),
-                lambda f: jnp.where(
-                    lane == LANES - 1, turned(f, r), pltpu.roll(values[f], LANES - 1, 1)
-                ),
-                lambda f: jnp.where(lane == 0, turned(f, r), pltpu.roll(values[f], 1, 1)),
-                coefs[0, r],
-                coefs[1, r],
-                coefs[2, r],
+                lambda f: pltpu.roll(values[f], LANES - 8, 1),
+                lambda f: pltpu.roll(values[f], 8, 1),
+                lambda f: pltpu.roll(values[f], LANES - 1, 1),
+                lambda f: pltpu.roll(values[f], 1, 1),
+                rim[0, fields, e],
+                rim[0, fields + 1, e],
+                rim[0, fields + 2, e],
             )
 
-        for r in range(k + 1, rows - k - 1, 2):
-
-            def store(i, f, value):
-                ref, at = place(k, r + i)
-                ref[f, at] = value
-
-            stencil(splat, [item(r), item(r + 1)], wall, store)
+        def inside():
+            values = [change[k - 1, f] for f in range(fields)]
+            return (
+                values,
+                lambda f: pltpu.roll(values[f], LANES - 8, 1),
+                lambda f: pltpu.roll(values[f], 8, 1),
+                lambda f: pltpu.roll(jnp.where(place == 4, rim[k, f, 1], values[f]), LANES - 1, 1),
+                lambda f: pltpu.roll(jnp.where(place == 3, rim[k, f, 0], values[f]), 1, 1),
+                own[fields],
+                own[fields + 1],
+                own[fields + 2],
+            )
+
+        items = [edge(0), edge(1)] if k + 1 < STEPS else []
+        edges = len(items)
+        if k:
+            items.append(inside())
+
+        def store(i, f, value):
+            if i < edges:
+                rim[k + 1, f, i] = value
+            else:
+                change[k, f] = value
+
+        stencil(splat, items, wall, store)
+
+    face = (lane < STEPS) | (lane >= LANES - STEPS)
 
     def products(f, totals):
         totals = list(totals)
         for x in range(2 * STEPS):
-            new = [krylov[k, f, x] for k in range(STEPS)]
+            new = []
+            for k in range(STEPS):
+                turned = pltpu.roll(change[k, f], LANES - (8 * (x + STEPS) + 4), 1)
+                new.append(made[k, f, x] + jnp.where(face, turned, 0.0))
+                krylov[k, f, x] = new[k]
             old = [held[m, f, x] for m in range(STEPS)]
             i = 0
             for a in range(STEPS):
@@ -426,14 +421,18 @@
     stream = ("outer", "inner")
     from_cross = lax.ppermute(cross, stream, swaps(outer * inner, 1))
     from_chip = lax.ppermute(chip, stream, swaps(outer * inner, 0))
-    own = pl.pallas_call(
-        own_edges_kernel,
-        out_shape=kept(everything, ny, nz),
-        in_specs=[VMEM] * 2,
-        out_specs=VMEM,
-        compiler_params=params,
-        name="own_edges",
-    )(*near(cross, chip))
+    own, splat, old_sums = pl.pallas_call(
+        prepare_kernel,
+        out_shape=(
+            kept(everything, ny, nz),
+            kept(fields * fields, ny, nz),
+            kept(len(PAIRS), ny, nz),
+        ),
+        in_specs=[SMEM] + [VMEM] * 3,
+        out_specs=(VMEM,) * 3,
+        compiler_params=params,
+        name="prepare",
+    )(mixing_matrix, *near(cross, chip, held))
     halves = kept((everything + 1) // 2, ny, nz)
     packed, to_right, to_left = pl.pallas_call(
         edges_kernel,
@@ -445,33 +444,30 @@
     )(*near(from_cross, from_chip, own))
     up, down = ring("span", span)
     from_left, from_right = up(to_right), down(to_left)
-    made, coefs, splat, old_sums = pl.pallas_call(
-        first_kernel,
-        out_shape=(
-            kept(fields, 4 * STEPS, ny, nz),
-            kept(EXTRA, 4 * STEPS, ny, nz),
-            kept(fields * fields, ny, nz),
-            kept(len(PAIRS), ny, nz),
-        ),
-        in_specs=[SMEM] + [VMEM] * 5,
-        out_specs=(VMEM,) * 4,
-        scratch_shapes=[pltpu.VMEM((everything, 4 * STEPS, ny, nz), jnp.float32)],
-        compiler_params=params,
-        name="first",
-    )(mixing_matrix, *near(from_cross, cross, chip, from_chip, held))
+    made = pl.pallas_call(
+        alone_kernel,
+        out_shape=kept(*vectors),
+        in_specs=[VMEM] * 5,
+        out_specs=VMEM,
+        scratch_shapes=[
+            pltpu.VMEM((everything, 4 * STEPS, ny, nz), jnp.float32),
+            pltpu.VMEM((2, fields, 2 * STEPS, ny, nz), jnp.float32),
+        ],
+        compiler_params=params,
+        name="alone",
+    )(*near(splat, from_cross, cross, chip, from_chip))
     krylov, sums = pl.pallas_call(
         krylov_kernel,
         out_shape=(kept(*vectors), kept(inner, 1, nz)),
-        in_specs=[VMEM] * 8,
+        in_specs=[VMEM] * 7,
         out_specs=(VMEM,) * 2,
         scratch_shapes=[
-            pltpu.VMEM((2, fields, 2 * STEPS, ny, nz), jnp.float32),
-            pltpu.VMEM((2, everything, 2, ny, nz), jnp.float32),
-            pltpu.VMEM((fields, ny, nz), jnp.float32),
+            pltpu.VMEM((STEPS, everything, 2, ny, nz), jnp.float32),
+            pltpu.VMEM((STEPS, fields, ny, nz), jnp.float32),
         ],
         compiler_params=params,
         name="krylov",
-    )(*near(splat, packed, from_left, from_right, made, coefs, held, old_sums))
+    )(*near(splat, packed, from_left, from_right, made, held, old_sums))
     sums = lax.all_to_all(sums, "inner", 0, 0, tiled=True)
     sums = jnp.broadcast_to(jnp.sum(sums, axis=0, keepdims=True), (outer * span, 1, nz))
     sums = lax.all_to_all(sums, ("outer", "span"), 0, 0, tiled=True)

time: 75.1 us -> 73.7 us (0.981)
  blocking collectives: 34.1 us -> 33.1 us
  waiting for transfers between devices: 0.88 us -> 0.01 us
    pallas_call x2, Pallas kernels: 1.97 us -> 3.83 us  [the longest x1 2.73 us: on_device(): pl.pallas_call(alone_kernel, out_shape=kept(*vectors), in_specs=[VMEM] *...]
    pallas_call x1, Pallas kernels: 2.85 us -> 1.46 us  [on_device(): pl.pallas_call(krylov_kernel, out_shape=(kept(*vectors), kept(inner, 1, n...]
    ppermute x1, waiting for transfers between devices: 0.87 us -> 0.01 us  [on_device(): from_chip = lax.ppermute(chip, stream, swaps(outer * inner, 0))]
  transfers between devices with their start and end apart: 4 -> 4, of which waited for: 1 -> 0; matrix products, arithmetic and copies ran while one was open for 0% -> 0% of each run, Pallas kernels for 3% -> 5%
where the time goes in v5:
time: 73.7 us; the launch traced here: 73.4 us
  blocking collectives  33.1 us (45%)
  starting transfers between devices  30.5 us (41%)
  Pallas kernels  9.01 us (12%)
  between operations  0.75 us (1%)
    ppermute x1, starting transfers between devices, on_device(): from_chip = lax.ppermute(chip, stream, swaps(outer * inner, 0))  18.6 us
    all_to_all x1, blocking collectives, on_device(): sums = lax.all_to_all(sums, ('outer', 'span'), 0, 0, tiled=True)  17.3 us
    all_to_all x1, blocking collectives, on_device(): sums = lax.all_to_all(sums, 'inner', 0, 0, tiled=True)  15.8 us
    ppermute x1, starting transfers between devices, on_device(): from_cross = lax.ppermute(cross, stream, swaps(outer * inner, 1))  5.39 us
    ppermute x1, starting transfers between devices, ring(): lax.ppermute(v, axes, down)  3.37 us
    ppermute x1, starting transfers between devices, ring(): lax.ppermute(v, axes, up)  3.11 us
    pallas_call x1, Pallas kernels, on_device(): pl.pallas_call(alone_kernel, out_shape=kept(*vectors), in_specs=[VMEM] *...  2.73 us
    pallas_call x1, Pallas kernels, on_device(): pl.pallas_call(functools.partial(finish_kernel, total), out_shape=(shape_...  1.82 us
  transfers between devices with their start and end apart: 4, of which 0 were waited for; matrix products, arithmetic and copies ran while one was open for 0% of the time, Pallas kernels for 5%

profile of v5, /device:TPU:1, one launch (start us, length us, event | category | flops | bytes accessed | tf_op | source)
XLA Modules:
  0.0 73.4 jit_solution(3061988617567950448)
XLA Ops:
  0.6 0.0 copy-start
  0.6 1.7 %start.1 = (f32[13,4,8,128]{3,2,1,0:T(8,128)S(1)}, f32[13,4,8,128]{3,2,1,0:T(8,128)S(1)}, f32[4,10,8,8,128]{4,3,2,1,0:T(8,128)S(1)}) custom-call(f32[4]{0:T(128)} %coeffs.1, f32[4,10,8,8,128]{4,3,2,1,0:T(8,128)} %basis.1, f32[8,8,128]{2,1,0:T(8,128)} %base_speed.1, f32[8,8,128]{2,1,0:T(8,128)} %span_speed.1, f32[8,8,128]{2,1,0:T(8,128)} %gain.1), custom_call_target="tpu_custom_call" | custom-call | tf_op jit(solution)/shard_map/start/pallas_call | solution.py:407
  2.3 5.4 %collective-permute-start = (f32[13,4,8,128]{3,2,1,0:T(8,128)S(1)}, f32[13,4,8,128]{3,2,1,0:T(8,128)S(1)}, u32[]{:S(2)}, u32[]{:S(2)}) collective-permute-start(f32[13,4,8,128]{3,2,1,0:T(8,128)S(1)} %get-tuple-element.14.cross), channel_id=1, source_target_pairs={{4,8},{12,16},{20,24},{28,32},{36,40},{44,48},{52,56},{60,64},{68,... | collective-permute-start | bytes 638984 | tf_op jit(solution)/shard_map/ppermute | solution.py:422
  7.7 18.6 %collective-permute-start.1 = (f32[13,4,8,128]{3,2,1,0:T(8,128)S(1)}, f32[13,4,8,128]{3,2,1,0:T(8,128)S(1)}, u32[]{:S(2)}, u32[]{:S(2)}) collective-permute-start(f32[13,4,8,128]{3,2,1,0:T(8,128)S(1)} %get-tuple-element.15.chip), channel_id=1, source_target_pairs={{0,4},{8,12},{16,20},{24,28},{32,36},{40,44},{48,52},{56,60},{64,6... | collective-permute-start | bytes 638984 | tf_op jit(solution)/shard_map/ppermute | solution.py:423
  26.3 0.0 copy-done
  26.3 1.1 %prepare.1 = (f32[13,8,128]{2,1,0:T(8,128)S(1)}, f32[100,8,128]{2,1,0:T(8,128)S(1)}, f32[10,8,128]{2,1,0:T(8,128)S(1)}) custom-call(f32[10,10]{1,0:T(8,128)S(1)} %copy-done, f32[13,4,8,128]{3,2,1,0:T(8,128)S(1)} %get-tuple-element.14.cross, f32[13,4,8,128]{3,2,1,0:T(8,128)S(1)} %get-tuple-element.15.chip, f32[4,10,8,8,128]{4,3,2,1,0:T(8,128)S(1)} %get-tuple-element.16.held.basis), custom_call_target="tpu_custom_call" | custom-call | tf_op jit(solution)/shard_map/prepare/pallas_call | solution.py:424
  27.4 0.0 collective-permute-done.from_cross
  27.4 0.0 collective-permute-done.1.from_chip
  27.4 0.2 edges.1
  27.7 3.1 %collective-permute-start.2 = (f32[7,8,128]{2,1,0:T(8,128)S(1)}, f32[7,8,128]{2,1,0:T(8,128)S(1)}, u32[]{:S(2)}, u32[]{:S(2)}) collective-permute-start(f32[7,8,128]{2,1,0:T(8,128)S(1)} %get-tuple-element.20), channel_id=1, source_target_pairs={{0,1},{1,2},{2,3},{3,0},{4,5},{5,6},{6,7},{7,4},{8,9},{9,10},{10,1... | collective-permute-start | bytes 86024 | tf_op jit(solution)/shard_map/ppermute | solution.py:384
  30.8 3.4 %collective-permute-start.3 = (f32[7,8,128]{2,1,0:T(8,128)S(1)}, f32[7,8,128]{2,1,0:T(8,128)S(1)}, u32[]{:S(2)}, u32[]{:S(2)}) collective-permute-start(f32[7,8,128]{2,1,0:T(8,128)S(1)} %get-tuple-element.21), channel_id=1, source_target_pairs={{1,0},{2,1},{3,2},{0,3},{5,4},{6,5},{7,6},{4,7},{9,8},{10,9},{11,1... | collective-permute-start | bytes 86024 | tf_op jit(solution)/shard_map/ppermute | solution.py:384
  34.2 2.7 %alone.1.made = f32[4,10,8,8,128]{4,3,2,1,0:T(8,128)S(1)} custom-call(f32[100,8,128]{2,1,0:T(8,128)S(1)} %get-tuple-element.17.splat, f32[13,4,8,128]{3,2,1,0:T(8,128)S(1)} %collective-permute-done.from_cross, f32[13,4,8,128]{3,2,1,0:T(8,128)S(1)} %get-tuple-element.14.cross, f32[13,4,8,128]{3,2,1,0:T(8,128)S(1)} %get-tuple-element.15.chip, ...), custom_call_target="tpu_custom_call" | custom-call | tf_op jit(solution)/shard_map/alone/pallas_call | solution.py:447
  36.9 0.0 collective-permute-done.2.from_left
  36.9 0.0 collective-permute-done.3.from_right
  36.9 1.5 %krylov.1 = (f32[4,10,8,8,128]{4,3,2,1,0:T(8,128)S(1)}, f32[32,1,128]{2,1,0:T(1,128)S(1)}) custom-call(f32[100,8,128]{2,1,0:T(8,128)S(1)} %get-tuple-element.17.splat, f32[13,8,128]{2,1,0:T(8,128)S(1)} %get-tuple-element.19.own, f32[7,8,128]{2,1,0:T(8,128)S(1)} %collective-permute-done.2.from_left, f32[7,8,128]{2,1,0:T(8,128)S(1)} %collective-permute-done.3.from_right, ...), custom_call_target="tpu_custom_call" | custom-call | tf_op jit(solution)/shard_map/krylov/pallas_call | solution.py:459
  38.4 15.8 %all_to_all.10 = f32[32,1,128]{2,1,0:T(1,128)S(1)} all-to-all(f32[32,1,128]{2,1,0:T(1,128)S(1)} %get-tuple-element.23), channel_id=1, replica_groups=mesh['outer'=8,'inner'=32,'span'=4] {'inner'}, dimensions={0} | all-to-all | bytes 32768 | tf_op jit(solution)/shard_map/all_to_all | solution.py:471
  54.2 0.1 reduce_sum.9
  54.3 17.3 %all_to_all.11.parts = f32[32,1,128]{2,1,0:T(1,128)S(1)} all-to-all(f32[32,1,128]{2,1,0:T(1,128)S(1)} %broadcast_in_dim.2), channel_id=1, replica_groups=mesh['outer'=8,'inner'=32,'span'=4] {'outer','span'}, dimensions={0} | all-to-all | bytes 32768 | tf_op jit(solution)/shard_map/all_to_all | solution.py:473
  71.6 1.8 %finish.1 = (f32[4,4]{1,0:T(4,128)}, f32[4,4]{1,0:T(4,128)}, f32[4,10,8,8,128]{4,3,2,1,0:T(8,128)}) custom-call(f32[32,1,128]{2,1,0:T(1,128)S(1)} %all_to_all.11.parts, f32[4,10,8,8,128]{4,3,2,1,0:T(8,128)S(1)} %get-tuple-element.24.krylov, f32[4,10,8,8,128]{4,3,2,1,0:T(8,128)S(1)} %get-tuple-element.16.held.basis), custom_call_target="tpu_custom_call" | custom-call | tf_op jit(solution)/shard_map/finish/pallas_call | solution.py:474
  (1 shorter events, 0.0 us)
Async XLA Ops:
  0.6 25.7 %copy-start = (f32[10,10]{1,0:T(8,128)S(1)}, f32[10,10]{1,0:T(8,128)}, u32[]{:S(2)}) copy-start(f32[10,10]{1,0:T(8,128)} %mixing.1) | copy-start | bytes 1204
  2.3 25.1 %collective-permute-start = (f32[13,4,8,128]{3,2,1,0:T(8,128)S(1)}, f32[13,4,8,128]{3,2,1,0:T(8,128)S(1)}, u32[]{:S(2)}, u32[]{:S(2)}) collective-permute-start(f32[13,4,8,128]{3,2,1,0:T(8,128)S(1)} %get-tuple-element.14.cross), channel_id=1, source_target_pairs={{4,8},{12,16},{20,24},{28,32},{36,40},{44,48},{52,56},{60,64},{68,... | collective-permute-start | bytes 638984 | tf_op jit(solution)/shard_map/ppermute | solution.py:422
  7.7 19.7 %collective-permute-start.1 = (f32[13,4,8,128]{3,2,1,0:T(8,128)S(1)}, f32[13,4,8,128]{3,2,1,0:T(8,128)S(1)}, u32[]{:S(2)}, u32[]{:S(2)}) collective-permute-start(f32[13,4,8,128]{3,2,1,0:T(8,128)S(1)} %get-tuple-element.15.chip), channel_id=1, source_target_pairs={{0,4},{8,12},{16,20},{24,28},{32,36},{40,44},{48,52},{56,60},{64,6... | collective-permute-start | bytes 638984 | tf_op jit(solution)/shard_map/ppermute | solution.py:423
  27.7 9.2 %collective-permute-start.2 = (f32[7,8,128]{2,1,0:T(8,128)S(1)}, f32[7,8,128]{2,1,0:T(8,128)S(1)}, u32[]{:S(2)}, u32[]{:S(2)}) collective-permute-start(f32[7,8,128]{2,1,0:T(8,128)S(1)} %get-tuple-element.20), channel_id=1, source_target_pairs={{0,1},{1,2},{2,3},{3,0},{4,5},{5,6},{6,7},{7,4},{8,9},{9,10},{10,1... | collective-permute-start | bytes 86024 | tf_op jit(solution)/shard_map/ppermute | solution.py:384
  30.8 6.1 %collective-permute-start.3 = (f32[7,8,128]{2,1,0:T(8,128)S(1)}, f32[7,8,128]{2,1,0:T(8,128)S(1)}, u32[]{:S(2)}, u32[]{:S(2)}) collective-permute-start(f32[7,8,128]{2,1,0:T(8,128)S(1)} %get-tuple-element.21), channel_id=1, source_target_pairs={{1,0},{2,1},{3,2},{0,3},{5,4},{6,5},{7,6},{4,7},{9,8},{10,9},{11,1... | collective-permute-start | bytes 86024 | tf_op jit(solution)/shard_map/ppermute | solution.py:384

commit v6 on v5

--- a/solution.py
+++ b/solution.py
@@ -1,4 +1,5 @@
 import functools
+import math
 
 import jax
 import jax.numpy as jnp
@@ -86,29 +87,6 @@
     return value
 
 
-def prepare_kernel(mixing, cross, chip, held, own, splat, old_sums):
-    fields, side = held.shape[1], STEPS * parity()
-    blank = jnp.zeros((8, LANES), jnp.float32)
-    for f in range(own.shape[0]):
-        rows = [(STEPS + side + r, cross[f, r]) for r in range(STEPS)]
-        rows += [(2 * STEPS - side + r, chip[f, r]) for r in range(STEPS)]
-        own[f] = pack(rows, blank)
-    for f in range(fields):
-        for g in range(fields):
-            splat[f * fields + g] = jnp.full((8, LANES), mixing[f, g], jnp.float32)
-
-    def products(f, totals):
-        totals = list(totals)
-        for x in range(2 * STEPS):
-            old = [held[m, f, x] for m in range(STEPS)]
-            for i, (a, b) in enumerate(PAIRS):
-                totals[i] = totals[i] + old[a] * old[b]
-        return tuple(totals)
-
-    for i, total in enumerate(lax.fori_loop(0, fields, products, (blank,) * len(PAIRS))):
-        old_sums[i] = total
-
-
 def edges_kernel(from_cross, from_chip, own, packed, to_right, to_left):
     side = 3 * STEPS * parity()
     made = []
@@ -156,9 +134,67 @@
             store(i, f, (near_x + near_z) + (near_y - 0.3 * v) + gain * mixed[i])
 
 
-def alone_kernel(splat, from_cross, cross, chip, from_chip, made, slabs, outer_rows):
+def advance(splat, tile, coef, rows, put):
+    fields, lane, wall = math.isqrt(splat.shape[0]), lane_index(), walls()
+
+    def item(r):
+        values = [tile(f, r) for f in range(fields)]
+        return (
+            values,
+            lambda f: tile(f, r + 1),
+            lambda f: tile(f, r - 1),
+            lambda f: jnp.where(lane == LANES - 1, 0.0, pltpu.roll(values[f], LANES - 1, 1)),
+            lambda f: jnp.where(lane == 0, 0.0, pltpu.roll(values[f], 1, 1)),
+            coef(0, r),
+            coef(1, r),
+            coef(2, r),
+        )
+
+    for pair in zip(rows[::2], rows[1::2]):
+
+        def store(i, f, value):
+            put(f, pair[i], value)
+
+        stencil(splat, [item(r) for r in pair], wall, store)
+
+
+def prepare_kernel(mixing, cross, chip, held, own, splat, old_sums, made, slabs):
+    fields, side = held.shape[1], STEPS * parity()
+    blank = jnp.zeros((8, LANES), jnp.float32)
+    for f in range(own.shape[0]):
+        rows = [(STEPS + side + r, cross[f, r]) for r in range(STEPS)]
+        rows += [(2 * STEPS - side + r, chip[f, r]) for r in range(STEPS)]
+        own[f] = pack(rows, blank)
+    for f in range(fields):
+        for g in range(fields):
+            splat[f * fields + g] = jnp.full((8, LANES), mixing[f, g], jnp.float32)
+    slabs[:, pl.ds(side, STEPS)] = cross[...]
+    slabs[:, pl.ds(STEPS - side, STEPS)] = chip[...]
+    for k in range(STEPS - 1):
+
+        def tile(f, r):
+            return made[k - 1, f, r] if k else slabs[f, r]
+
+        def store(f, r, value):
+            made[k, f, r] = value
+
+        rows = list(range(k + 1, 2 * STEPS - k - 1))
+        advance(splat, tile, lambda e, r: slabs[fields + e, r], rows, store)
+
+    def products(f, totals):
+        totals = list(totals)
+        for x in range(2 * STEPS):
+            old = [held[m, f, x] for m in range(STEPS)]
+            for i, (a, b) in enumerate(PAIRS):
+                totals[i] = totals[i] + old[a] * old[b]
+        return tuple(totals)
+
+    for i, total in enumerate(lax.fori_loop(0, fields, products, (blank,) * len(PAIRS))):
+        old_sums[i] = total
+
+
+def alone_kernel(splat, from_cross, cross, chip, from_chip, ahead, made, slabs, outer_rows):
     fields, rows = cross.shape[0] - EXTRA, 4 * STEPS
-    lane, wall = lane_index(), walls()
     side = STEPS * parity()
     for ref, row in (
         (from_cross, 3 * side),
@@ -168,39 +204,26 @@
     ):
         slabs[:, pl.ds(row, STEPS)] = ref[...]
 
-    def place(k, r):
-        if k < 0:
-            return slabs, r
-        if STEPS <= r < 3 * STEPS:
-            return made.at[k], r - STEPS
-        return outer_rows.at[k % 2], r if r < STEPS else r - 2 * STEPS
+    def done(k, r):
+        return STEPS + k < r < 3 * STEPS - k - 1
 
     for k in range(STEPS):
 
         def tile(f, r):
-            ref, at = place(k - 1, r)
-            return ref[f, at]
-
-        def item(r):
-            values = [tile(f, r) for f in range(fields)]
-            return (
-                values,
-                lambda f: tile(f, r + 1),
-                lambda f: tile(f, r - 1),
-                lambda f: jnp.where(lane == LANES - 1, 0.0, pltpu.roll(values[f], LANES - 1, 1)),
-                lambda f: jnp.where(lane == 0, 0.0, pltpu.roll(values[f], 1, 1)),
-                slabs[fields, r],
-                slabs[fields + 1, r],
-                slabs[fields + 2, r],
-            )
-
-        for r in range(k + 1, rows - k - 1, 2):
-
-            def store(i, f, value):
-                ref, at = place(k, r + i)
-                ref[f, at] = value
-
-            stencil(splat, [item(r), item(r + 1)], wall, store)
+            if k == 0:
+                return slabs[f, r]
+            if STEPS <= r < 3 * STEPS:
+                return (ahead if done(k - 1, r) else made)[k - 1, f, r - STEPS]
+            return outer_rows[(k - 1) % 2, f, r if r < STEPS else r - 2 * STEPS]
+
+        def put(f, r, value):
+            if STEPS <= r < 3 * STEPS:
+                made[k, f, r - STEPS] = value
+            else:
+                outer_rows[k % 2, f, r if r < STEPS else r - 2 * STEPS] = value
+
+        left = [r for r in range(k + 1, rows - k - 1) if not done(k, r)]
+        advance(splat, tile, lambda e, r: slabs[fields + e, r], left, put)
 
 
 def krylov_kernel(
@@ -421,15 +444,17 @@
     stream = ("outer", "inner")
     from_cross = lax.ppermute(cross, stream, swaps(outer * inner, 1))
     from_chip = lax.ppermute(chip, stream, swaps(outer * inner, 0))
-    own, splat, old_sums = pl.pallas_call(
+    own, splat, old_sums, ahead = pl.pallas_call(
         prepare_kernel,
         out_shape=(
             kept(everything, ny, nz),
             kept(fields * fields, ny, nz),
             kept(len(PAIRS), ny, nz),
+            kept(*vectors),
         ),
         in_specs=[SMEM] + [VMEM] * 3,
-        out_specs=(VMEM,) * 3,
+        out_specs=(VMEM,) * 4,
+        scratch_shapes=[pltpu.VMEM((everything, 2 * STEPS, ny, nz), jnp.float32)],
         compiler_params=params,
         name="prepare",
     )(mixing_matrix, *near(cross, chip, held))
@@ -447,15 +472,16 @@
     made = pl.pallas_call(
         alone_kernel,
         out_shape=kept(*vectors),
-        in_specs=[VMEM] * 5,
+        in_specs=[VMEM] * 6,
         out_specs=VMEM,
+        input_output_aliases={5: 0},
         scratch_shapes=[
             pltpu.VMEM((everything, 4 * STEPS, ny, nz), jnp.float32),
             pltpu.VMEM((2, fields, 2 * STEPS, ny, nz), jnp.float32),
         ],
         compiler_params=params,
         name="alone",
-    )(*near(splat, from_cross, cross, chip, from_chip))
+    )(*near(splat, from_cross, cross, chip, from_chip, ahead))
     krylov, sums = pl.pallas_call(
         krylov_kernel,
         out_shape=(kept(*vectors), kept(inner, 1, nz)),

time: 73.7 us -> 73.7 us (level)
    pallas_call x1, Pallas kernels: 2.73 us -> 1.94 us  [on_device(): pl.pallas_call(alone_kernel, out_shape=kept(*vectors), in_specs=[VMEM] *...]
where the time goes in v6:
time: 73.7 us; the launch traced here: 73.4 us
  blocking collectives  33.2 us (45%)
  starting transfers between devices  30.5 us (41%)
  Pallas kernels  8.83 us (12%)
  between operations  0.75 us (1%)
    ppermute x1, starting transfers between devices, on_device(): from_chip = lax.ppermute(chip, stream, swaps(outer * inner, 0))  18.6 us
    all_to_all x1, blocking collectives, on_device(): sums = lax.all_to_all(sums, ('outer', 'span'), 0, 0, tiled=True)  18 us
    all_to_all x1, blocking collectives, on_device(): sums = lax.all_to_all(sums, 'inner', 0, 0, tiled=True)  15.3 us
    ppermute x1, starting transfers between devices, on_device(): from_cross = lax.ppermute(cross, stream, swaps(outer * inner, 1))  5.39 us
    ppermute x1, starting transfers between devices, ring(): lax.ppermute(v, axes, down)  3.37 us
    ppermute x1, starting transfers between devices, ring(): lax.ppermute(v, axes, up)  3.11 us
    pallas_call x1, Pallas kernels, on_device(): pl.pallas_call(alone_kernel, out_shape=kept(*vectors), in_specs=[VMEM] *...  1.94 us
    pallas_call x1, Pallas kernels, on_device(): pl.pallas_call(functools.partial(finish_kernel, total), out_shape=(shape_...  1.82 us
  transfers between devices with their start and end apart: 4, of which 0 were waited for; matrix products, arithmetic and copies ran while one was open for 0% of the time, Pallas kernels for 5%

profile of v6, /device:TPU:1, one launch (start us, length us, event | category | flops | bytes accessed | tf_op | source)
XLA Modules:
  0.0 73.4 jit_solution(6559329713051353293)
XLA Ops:
  0.6 0.0 copy-start
  0.6 1.7 %start.1 = (f32[13,4,8,128]{3,2,1,0:T(8,128)S(1)}, f32[13,4,8,128]{3,2,1,0:T(8,128)S(1)}, f32[4,10,8,8,128]{4,3,2,1,0:T(8,128)S(1)}) custom-call(f32[4]{0:T(128)} %coeffs.1, f32[4,10,8,8,128]{4,3,2,1,0:T(8,128)} %basis.1, f32[8,8,128]{2,1,0:T(8,128)} %base_speed.1, f32[8,8,128]{2,1,0:T(8,128)} %span_speed.1, f32[8,8,128]{2,1,0:T(8,128)} %gain.1), custom_call_target="tpu_custom_call" | custom-call | tf_op jit(solution)/shard_map/start/pallas_call | solution.py:430
  2.3 5.4 %collective-permute-start = (f32[13,4,8,128]{3,2,1,0:T(8,128)S(1)}, f32[13,4,8,128]{3,2,1,0:T(8,128)S(1)}, u32[]{:S(2)}, u32[]{:S(2)}) collective-permute-start(f32[13,4,8,128]{3,2,1,0:T(8,128)S(1)} %get-tuple-element.15.cross), channel_id=1, source_target_pairs={{4,8},{12,16},{20,24},{28,32},{36,40},{44,48},{52,56},{60,64},{68,... | collective-permute-start | bytes 638984 | tf_op jit(solution)/shard_map/ppermute | solution.py:445
  7.7 18.6 %collective-permute-start.1 = (f32[13,4,8,128]{3,2,1,0:T(8,128)S(1)}, f32[13,4,8,128]{3,2,1,0:T(8,128)S(1)}, u32[]{:S(2)}, u32[]{:S(2)}) collective-permute-start(f32[13,4,8,128]{3,2,1,0:T(8,128)S(1)} %get-tuple-element.16.chip), channel_id=1, source_target_pairs={{0,4},{8,12},{16,20},{24,28},{32,36},{40,44},{48,52},{56,60},{64,6... | collective-permute-start | bytes 638984 | tf_op jit(solution)/shard_map/ppermute | solution.py:446
  26.3 0.0 copy-done
  26.3 1.8 %prepare.1 = (f32[13,8,128]{2,1,0:T(8,128)S(1)}, f32[100,8,128]{2,1,0:T(8,128)S(1)}, f32[10,8,128]{2,1,0:T(8,128)S(1)}, f32[4,10,8,8,128]{4,3,2,1,0:T(8,128)S(1)}) custom-call(f32[10,10]{1,0:T(8,128)S(1)} %copy-done, f32[13,4,8,128]{3,2,1,0:T(8,128)S(1)} %get-tuple-element.15.cross, f32[13,4,8,128]{3,2,1,0:T(8,128)S(1)} %get-tuple-element.16.chip, ...), custom_call_target="tpu_custom_call" | custom-call | tf_op jit(solution)/shard_map/prepare/pallas_call | solution.py:447
  28.1 0.0 collective-permute-done.from_cross
  28.1 0.0 collective-permute-done.1.from_chip
  28.1 0.2 edges.1
  28.3 3.1 %collective-permute-start.2 = (f32[7,8,128]{2,1,0:T(8,128)S(1)}, f32[7,8,128]{2,1,0:T(8,128)S(1)}, u32[]{:S(2)}, u32[]{:S(2)}) collective-permute-start(f32[7,8,128]{2,1,0:T(8,128)S(1)} %get-tuple-element.21), channel_id=1, source_target_pairs={{0,1},{1,2},{2,3},{3,0},{4,5},{5,6},{6,7},{7,4},{8,9},{9,10},{10,1... | collective-permute-start | bytes 86024 | tf_op jit(solution)/shard_map/ppermute | solution.py:407
  31.5 3.4 %collective-permute-start.3 = (f32[7,8,128]{2,1,0:T(8,128)S(1)}, f32[7,8,128]{2,1,0:T(8,128)S(1)}, u32[]{:S(2)}, u32[]{:S(2)}) collective-permute-start(f32[7,8,128]{2,1,0:T(8,128)S(1)} %get-tuple-element.22), channel_id=1, source_target_pairs={{1,0},{2,1},{3,2},{0,3},{5,4},{6,5},{7,6},{4,7},{9,8},{10,9},{11,1... | collective-permute-start | bytes 86024 | tf_op jit(solution)/shard_map/ppermute | solution.py:407
  34.8 1.9 %alone.1.made = f32[4,10,8,8,128]{4,3,2,1,0:T(8,128)S(1)} custom-call(f32[100,8,128]{2,1,0:T(8,128)S(1)} %get-tuple-element.18.splat, f32[13,4,8,128]{3,2,1,0:T(8,128)S(1)} %collective-permute-done.from_cross, f32[13,4,8,128]{3,2,1,0:T(8,128)S(1)} %get-tuple-element.15.cross, ...), custom_call_target="tpu_custom_call", output_to_operand_aliasing={{}: (5, {})} | custom-call | tf_op jit(solution)/shard_map/alone/pallas_call | solution.py:472
  36.8 0.0 collective-permute-done.2.from_left
  36.8 0.0 collective-permute-done.3.from_right
  36.8 1.4 %krylov.1 = (f32[4,10,8,8,128]{4,3,2,1,0:T(8,128)S(1)}, f32[32,1,128]{2,1,0:T(1,128)S(1)}) custom-call(f32[100,8,128]{2,1,0:T(8,128)S(1)} %get-tuple-element.18.splat, f32[13,8,128]{2,1,0:T(8,128)S(1)} %get-tuple-element.20.own, f32[7,8,128]{2,1,0:T(8,128)S(1)} %collective-permute-done.2.from_left, f32[7,8,128]{2,1,0:T(8,128)S(1)} %collective-permute-done.3.from_right, ...), custom_call_target="tpu_custom_call" | custom-call | tf_op jit(solution)/shard_map/krylov/pallas_call | solution.py:485
  38.2 15.3 %all_to_all.10 = f32[32,1,128]{2,1,0:T(1,128)S(1)} all-to-all(f32[32,1,128]{2,1,0:T(1,128)S(1)} %get-tuple-element.25), channel_id=1, replica_groups=mesh['outer'=8,'inner'=32,'span'=4] {'inner'}, dimensions={0} | all-to-all | bytes 32768 | tf_op jit(solution)/shard_map/all_to_all | solution.py:497
  53.5 0.1 reduce_sum.9
  53.6 18.0 %all_to_all.11.parts = f32[32,1,128]{2,1,0:T(1,128)S(1)} all-to-all(f32[32,1,128]{2,1,0:T(1,128)S(1)} %broadcast_in_dim.2), channel_id=1, replica_groups=mesh['outer'=8,'inner'=32,'span'=4] {'outer','span'}, dimensions={0} | all-to-all | bytes 32768 | tf_op jit(solution)/shard_map/all_to_all | solution.py:499
  71.5 1.8 %finish.1 = (f32[4,4]{1,0:T(4,128)}, f32[4,4]{1,0:T(4,128)}, f32[4,10,8,8,128]{4,3,2,1,0:T(8,128)}) custom-call(f32[32,1,128]{2,1,0:T(1,128)S(1)} %all_to_all.11.parts, f32[4,10,8,8,128]{4,3,2,1,0:T(8,128)S(1)} %get-tuple-element.26.krylov, f32[4,10,8,8,128]{4,3,2,1,0:T(8,128)S(1)} %get-tuple-element.17.held.basis), custom_call_target="tpu_custom_call" | custom-call | tf_op jit(solution)/shard_map/finish/pallas_call | solution.py:500
  (1 shorter events, 0.0 us)
Async XLA Ops:
  0.6 25.7 %copy-start = (f32[10,10]{1,0:T(8,128)S(1)}, f32[10,10]{1,0:T(8,128)}, u32[]{:S(2)}) copy-start(f32[10,10]{1,0:T(8,128)} %mixing.1) | copy-start | bytes 1204
  2.3 25.8 %collective-permute-start = (f32[13,4,8,128]{3,2,1,0:T(8,128)S(1)}, f32[13,4,8,128]{3,2,1,0:T(8,128)S(1)}, u32[]{:S(2)}, u32[]{:S(2)}) collective-permute-start(f32[13,4,8,128]{3,2,1,0:T(8,128)S(1)} %get-tuple-element.15.cross), channel_id=1, source_target_pairs={{4,8},{12,16},{20,24},{28,32},{36,40},{44,48},{52,56},{60,64},{68,... | collective-permute-start | bytes 638984 | tf_op jit(solution)/shard_map/ppermute | solution.py:445
  7.7 20.4 %collective-permute-start.1 = (f32[13,4,8,128]{3,2,1,0:T(8,128)S(1)}, f32[13,4,8,128]{3,2,1,0:T(8,128)S(1)}, u32[]{:S(2)}, u32[]{:S(2)}) collective-permute-start(f32[13,4,8,128]{3,2,1,0:T(8,128)S(1)} %get-tuple-element.16.chip), channel_id=1, source_target_pairs={{0,4},{8,12},{16,20},{24,28},{32,36},{40,44},{48,52},{56,60},{64,6... | collective-permute-start | bytes 638984 | tf_op jit(solution)/shard_map/ppermute | solution.py:446
  28.3 8.5 %collective-permute-start.2 = (f32[7,8,128]{2,1,0:T(8,128)S(1)}, f32[7,8,128]{2,1,0:T(8,128)S(1)}, u32[]{:S(2)}, u32[]{:S(2)}) collective-permute-start(f32[7,8,128]{2,1,0:T(8,128)S(1)} %get-tuple-element.21), channel_id=1, source_target_pairs={{0,1},{1,2},{2,3},{3,0},{4,5},{5,6},{6,7},{7,4},{8,9},{9,10},{10,1... | collective-permute-start | bytes 86024 | tf_op jit(solution)/shard_map/ppermute | solution.py:407
  31.5 5.3 %collective-permute-start.3 = (f32[7,8,128]{2,1,0:T(8,128)S(1)}, f32[7,8,128]{2,1,0:T(8,128)S(1)}, u32[]{:S(2)}, u32[]{:S(2)}) collective-permute-start(f32[7,8,128]{2,1,0:T(8,128)S(1)} %get-tuple-element.22), channel_id=1, source_target_pairs={{1,0},{2,1},{3,2},{0,3},{5,4},{6,5},{7,6},{4,7},{9,8},{10,9},{11,1... | collective-permute-start | bytes 86024 | tf_op jit(solution)/shard_map/ppermute | solution.py:407

commit v7 on v6

--- a/solution.py
+++ b/solution.py
@@ -389,7 +389,8 @@
                 new_out[k, f, x] = made[k]
         return carry
 
-    lax.fori_loop(0, fields, field, 0)
+    for f in range(fields):
+        field(f, 0)
 
 
 def far(*arrays):

time: 73.7 us -> 74 us (level)
  no operation moved by 1% of the time
where the time goes in v7:
time: 74 us; the launch traced here: 73.7 us
  blocking collectives  33.2 us (45%)
  starting transfers between devices  30.5 us (41%)
  Pallas kernels  9.13 us (12%)
  between operations  0.75 us (1%)
    ppermute x1, starting transfers between devices, on_device(): from_chip = lax.ppermute(chip, stream, swaps(outer * inner, 0))  18.6 us
    all_to_all x1, blocking collectives, on_device(): sums = lax.all_to_all(sums, ('outer', 'span'), 0, 0, tiled=True)  18 us
    all_to_all x1, blocking collectives, on_device(): sums = lax.all_to_all(sums, 'inner', 0, 0, tiled=True)  15.3 us
    ppermute x1, starting transfers between devices, on_device(): from_cross = lax.ppermute(cross, stream, swaps(outer * inner, 1))  5.39 us
    ppermute x1, starting transfers between devices, ring(): lax.ppermute(v, axes, down)  3.37 us
    ppermute x1, starting transfers between devices, ring(): lax.ppermute(v, axes, up)  3.11 us
    pallas_call x1, Pallas kernels, on_device(): pl.pallas_call(functools.partial(finish_kernel, total), out_shape=(shape_...  2.13 us
    pallas_call x1, Pallas kernels, on_device(): pl.pallas_call(alone_kernel, out_shape=kept(*vectors), in_specs=[VMEM] *...  1.94 us
  transfers between devices with their start and end apart: 4, of which 0 were waited for; matrix products, arithmetic and copies ran while one was open for 0% of the time, Pallas kernels for 5%

profile of v7, /device:TPU:1, one launch (start us, length us, event | category | flops | bytes accessed | tf_op | source)
XLA Modules:
  0.0 73.7 jit_solution(2385174078446153595)
XLA Ops:
  0.6 0.0 copy-start
  0.6 1.7 %start.1 = (f32[13,4,8,128]{3,2,1,0:T(8,128)S(1)}, f32[13,4,8,128]{3,2,1,0:T(8,128)S(1)}, f32[4,10,8,8,128]{4,3,2,1,0:T(8,128)S(1)}) custom-call(f32[4]{0:T(128)} %coeffs.1, f32[4,10,8,8,128]{4,3,2,1,0:T(8,128)} %basis.1, f32[8,8,128]{2,1,0:T(8,128)} %base_speed.1, f32[8,8,128]{2,1,0:T(8,128)} %span_speed.1, f32[8,8,128]{2,1,0:T(8,128)} %gain.1), custom_call_target="tpu_custom_call" | custom-call | tf_op jit(solution)/shard_map/start/pallas_call | solution.py:431
  2.3 5.4 %collective-permute-start = (f32[13,4,8,128]{3,2,1,0:T(8,128)S(1)}, f32[13,4,8,128]{3,2,1,0:T(8,128)S(1)}, u32[]{:S(2)}, u32[]{:S(2)}) collective-permute-start(f32[13,4,8,128]{3,2,1,0:T(8,128)S(1)} %get-tuple-element.15.cross), channel_id=1, source_target_pairs={{4,8},{12,16},{20,24},{28,32},{36,40},{44,48},{52,56},{60,64},{68,... | collective-permute-start | bytes 638984 | tf_op jit(solution)/shard_map/ppermute | solution.py:446
  7.7 18.6 %collective-permute-start.1 = (f32[13,4,8,128]{3,2,1,0:T(8,128)S(1)}, f32[13,4,8,128]{3,2,1,0:T(8,128)S(1)}, u32[]{:S(2)}, u32[]{:S(2)}) collective-permute-start(f32[13,4,8,128]{3,2,1,0:T(8,128)S(1)} %get-tuple-element.16.chip), channel_id=1, source_target_pairs={{0,4},{8,12},{16,20},{24,28},{32,36},{40,44},{48,52},{56,60},{64,6... | collective-permute-start | bytes 638984 | tf_op jit(solution)/shard_map/ppermute | solution.py:447
  26.3 0.0 copy-done
  26.3 1.8 %prepare.1 = (f32[13,8,128]{2,1,0:T(8,128)S(1)}, f32[100,8,128]{2,1,0:T(8,128)S(1)}, f32[10,8,128]{2,1,0:T(8,128)S(1)}, f32[4,10,8,8,128]{4,3,2,1,0:T(8,128)S(1)}) custom-call(f32[10,10]{1,0:T(8,128)S(1)} %copy-done, f32[13,4,8,128]{3,2,1,0:T(8,128)S(1)} %get-tuple-element.15.cross, f32[13,4,8,128]{3,2,1,0:T(8,128)S(1)} %get-tuple-element.16.chip, ...), custom_call_target="tpu_custom_call" | custom-call | tf_op jit(solution)/shard_map/prepare/pallas_call | solution.py:448
  28.1 0.0 collective-permute-done.from_cross
  28.1 0.0 collective-permute-done.1.from_chip
  28.1 0.2 edges.1
  28.3 3.1 %collective-permute-start.2 = (f32[7,8,128]{2,1,0:T(8,128)S(1)}, f32[7,8,128]{2,1,0:T(8,128)S(1)}, u32[]{:S(2)}, u32[]{:S(2)}) collective-permute-start(f32[7,8,128]{2,1,0:T(8,128)S(1)} %get-tuple-element.21), channel_id=1, source_target_pairs={{0,1},{1,2},{2,3},{3,0},{4,5},{5,6},{6,7},{7,4},{8,9},{9,10},{10,1... | collective-permute-start | bytes 86024 | tf_op jit(solution)/shard_map/ppermute | solution.py:408
  31.5 3.4 %collective-permute-start.3 = (f32[7,8,128]{2,1,0:T(8,128)S(1)}, f32[7,8,128]{2,1,0:T(8,128)S(1)}, u32[]{:S(2)}, u32[]{:S(2)}) collective-permute-start(f32[7,8,128]{2,1,0:T(8,128)S(1)} %get-tuple-element.22), channel_id=1, source_target_pairs={{1,0},{2,1},{3,2},{0,3},{5,4},{6,5},{7,6},{4,7},{9,8},{10,9},{11,1... | collective-permute-start | bytes 86024 | tf_op jit(solution)/shard_map/ppermute | solution.py:408
  34.8 1.9 %alone.1.made = f32[4,10,8,8,128]{4,3,2,1,0:T(8,128)S(1)} custom-call(f32[100,8,128]{2,1,0:T(8,128)S(1)} %get-tuple-element.18.splat, f32[13,4,8,128]{3,2,1,0:T(8,128)S(1)} %collective-permute-done.from_cross, f32[13,4,8,128]{3,2,1,0:T(8,128)S(1)} %get-tuple-element.15.cross, ...), custom_call_target="tpu_custom_call", output_to_operand_aliasing={{}: (5, {})} | custom-call | tf_op jit(solution)/shard_map/alone/pallas_call | solution.py:473
  36.8 0.0 collective-permute-done.2.from_left
  36.8 0.0 collective-permute-done.3.from_right
  36.8 1.4 %krylov.1 = (f32[4,10,8,8,128]{4,3,2,1,0:T(8,128)S(1)}, f32[32,1,128]{2,1,0:T(1,128)S(1)}) custom-call(f32[100,8,128]{2,1,0:T(8,128)S(1)} %get-tuple-element.18.splat, f32[13,8,128]{2,1,0:T(8,128)S(1)} %get-tuple-element.20.own, f32[7,8,128]{2,1,0:T(8,128)S(1)} %collective-permute-done.2.from_left, f32[7,8,128]{2,1,0:T(8,128)S(1)} %collective-permute-done.3.from_right, ...), custom_call_target="tpu_custom_call" | custom-call | tf_op jit(solution)/shard_map/krylov/pallas_call | solution.py:486
  38.2 15.3 %all_to_all.10 = f32[32,1,128]{2,1,0:T(1,128)S(1)} all-to-all(f32[32,1,128]{2,1,0:T(1,128)S(1)} %get-tuple-element.25), channel_id=1, replica_groups=mesh['outer'=8,'inner'=32,'span'=4] {'inner'}, dimensions={0} | all-to-all | bytes 32768 | tf_op jit(solution)/shard_map/all_to_all | solution.py:498
  53.5 0.1 reduce_sum.9
  53.6 18.0 %all_to_all.11.parts = f32[32,1,128]{2,1,0:T(1,128)S(1)} all-to-all(f32[32,1,128]{2,1,0:T(1,128)S(1)} %broadcast_in_dim.2), channel_id=1, replica_groups=mesh['outer'=8,'inner'=32,'span'=4] {'outer','span'}, dimensions={0} | all-to-all | bytes 32768 | tf_op jit(solution)/shard_map/all_to_all | solution.py:500
  71.5 2.1 %finish.1 = (f32[4,4]{1,0:T(4,128)}, f32[4,4]{1,0:T(4,128)}, f32[4,10,8,8,128]{4,3,2,1,0:T(8,128)}) custom-call(f32[32,1,128]{2,1,0:T(1,128)S(1)} %all_to_all.11.parts, f32[4,10,8,8,128]{4,3,2,1,0:T(8,128)S(1)} %get-tuple-element.26.krylov, f32[4,10,8,8,128]{4,3,2,1,0:T(8,128)S(1)} %get-tuple-element.17.held.basis), custom_call_target="tpu_custom_call" | custom-call | tf_op jit(solution)/shard_map/finish/pallas_call | solution.py:501
  (1 shorter events, 0.0 us)
Async XLA Ops:
  0.6 25.7 %copy-start = (f32[10,10]{1,0:T(8,128)S(1)}, f32[10,10]{1,0:T(8,128)}, u32[]{:S(2)}) copy-start(f32[10,10]{1,0:T(8,128)} %mixing.1) | copy-start | bytes 1204
  2.3 25.8 %collective-permute-start = (f32[13,4,8,128]{3,2,1,0:T(8,128)S(1)}, f32[13,4,8,128]{3,2,1,0:T(8,128)S(1)}, u32[]{:S(2)}, u32[]{:S(2)}) collective-permute-start(f32[13,4,8,128]{3,2,1,0:T(8,128)S(1)} %get-tuple-element.15.cross), channel_id=1, source_target_pairs={{4,8},{12,16},{20,24},{28,32},{36,40},{44,48},{52,56},{60,64},{68,... | collective-permute-start | bytes 638984 | tf_op jit(solution)/shard_map/ppermute | solution.py:446
  7.7 20.4 %collective-permute-start.1 = (f32[13,4,8,128]{3,2,1,0:T(8,128)S(1)}, f32[13,4,8,128]{3,2,1,0:T(8,128)S(1)}, u32[]{:S(2)}, u32[]{:S(2)}) collective-permute-start(f32[13,4,8,128]{3,2,1,0:T(8,128)S(1)} %get-tuple-element.16.chip), channel_id=1, source_target_pairs={{0,4},{8,12},{16,20},{24,28},{32,36},{40,44},{48,52},{56,60},{64,6... | collective-permute-start | bytes 638984 | tf_op jit(solution)/shard_map/ppermute | solution.py:447
  28.3 8.5 %collective-permute-start.2 = (f32[7,8,128]{2,1,0:T(8,128)S(1)}, f32[7,8,128]{2,1,0:T(8,128)S(1)}, u32[]{:S(2)}, u32[]{:S(2)}) collective-permute-start(f32[7,8,128]{2,1,0:T(8,128)S(1)} %get-tuple-element.21), channel_id=1, source_target_pairs={{0,1},{1,2},{2,3},{3,0},{4,5},{5,6},{6,7},{7,4},{8,9},{9,10},{10,1... | collective-permute-start | bytes 86024 | tf_op jit(solution)/shard_map/ppermute | solution.py:408
  31.5 5.3 %collective-permute-start.3 = (f32[7,8,128]{2,1,0:T(8,128)S(1)}, f32[7,8,128]{2,1,0:T(8,128)S(1)}, u32[]{:S(2)}, u32[]{:S(2)}) collective-permute-start(f32[7,8,128]{2,1,0:T(8,128)S(1)} %get-tuple-element.22), channel_id=1, source_target_pairs={{1,0},{2,1},{3,2},{0,3},{5,4},{6,5},{7,6},{4,7},{9,8},{10,9},{11,1... | collective-permute-start | bytes 86024 | tf_op jit(solution)/shard_map/ppermute | solution.py:408
